TPU v7x, 32 devices: a whole 2x2x4 slice. The times are simulated.
32 devices in a mesh: fsdp: 8 (over y, x, core), seq: 4 (over z).
Axes of the slice: x: 2, y: 2, z: 4, core: 2. Of those that a mesh axis runs over, the one named last changes fastest.
Arguments:
- tokens: bfloat16 [8192, 768], P(('fsdp', 'seq')), may hold values from -6 to 6
- memory: bfloat16 [8, 20, 768], P('fsdp'), may hold values from -6 to 6
- lengths: int32 [8], P('fsdp'), may hold values from 256 to 1004, as said below
- w_qkv: bfloat16 [2, 768, 2304], P(None, 'fsdp'), may hold values from -0.21875 to 0.21875
- b_qv: bfloat16 [2, 1536], P(None, 'fsdp'), may hold values from -1.5 to 1.5
- w_out: bfloat16 [2, 768, 768], P(None, 'fsdp'), may hold values from -2 to 2
- b_out: bfloat16 [2, 768], P(None, 'fsdp'), may hold values from -1.5 to 1.5
- gain_attn: bfloat16 [2, 768], P(None, 'fsdp'), may hold values from 0.5 to 1.5
- shift_attn: bfloat16 [2, 768], P(None, 'fsdp'), may hold values from -1.5 to 1.5
- w_up: bfloat16 [2, 768, 3072], P(None, 'fsdp'), may hold values from -0.21875 to 0.21875
- b_up: bfloat16 [2, 3072], P(None, 'fsdp'), may hold values from -1.5 to 1.5
- w_down: bfloat16 [2, 3072, 768], P(None, 'fsdp'), may hold values from -0.109375 to 0.109375
- b_down: bfloat16 [2, 768], P(None, 'fsdp'), may hold values from -1.5 to 1.5
- gain_ffn: bfloat16 [2, 768], P(None, 'fsdp'), may hold values from 0.5 to 1.5
- shift_ffn: bfloat16 [2, 768], P(None, 'fsdp'), may hold values from -1.5 to 1.5
- cotangent: float32 [8192, 768], P(('fsdp', 'seq')), may hold values from -6 to 6
Outputs:
- result: float32 [8192, 768], P(('fsdp', 'seq'))
- grad_tokens: float32 [8192, 768], P(('fsdp', 'seq'))
- grad_memory: float32 [8, 20, 768], P('fsdp')
- grad_w_qkv: float32 [2, 768, 2304], P(None, 'fsdp')
- grad_b_qv: float32 [2, 1536], P(None, 'fsdp')
- grad_w_out: float32 [2, 768, 768], P(None, 'fsdp')
- grad_b_out: float32 [2, 768], P(None, 'fsdp')
- grad_gain_attn: float32 [2, 768], P(None, 'fsdp')
- grad_shift_attn: float32 [2, 768], P(None, 'fsdp')
- grad_w_up: float32 [2, 768, 3072], P(None, 'fsdp')
- grad_b_up: float32 [2, 3072], P(None, 'fsdp')
- grad_w_down: float32 [2, 3072, 768], P(None, 'fsdp')
- grad_b_down: float32 [2, 768], P(None, 'fsdp')
- grad_gain_ffn: float32 [2, 768], P(None, 'fsdp')
- grad_shift_ffn: float32 [2, 768], P(None, 'fsdp')
Inputs may be any that keep to these rules, and one draw needn't show every extreme that they name: `lengths`: one sequence has exactly 1004 token rows and another exactly 256.
All inputs are finite; a program needn't handle non-finite values.
Results may differ from a plain program's by a relative error of at most 0.018.
Values may be sent and summed in bfloat16 or wider, within the bound.
A program may use at most 192 MiB of HBM per device.

v0:
```python
import math

import jax
import jax.numpy as jnp
from jax import lax
from jax.sharding import PartitionSpec as P

D = 768
HEADS = 12
HD = 64
MEM = 10
LAYERS = 2


norm_eps = 1e-12
masked_score = -1e30


def norm_rows(values, gain_vec, shift_vec):
    row_mean = jnp.mean(values, axis=-1, keepdims=True)
    centred = values - row_mean
    variance = jnp.mean(centred * centred, axis=-1, keepdims=True)
    return centred * lax.rsqrt(variance + norm_eps) * gain_vec + shift_vec


def gelu_exact(values):
    return jax.nn.gelu(values, approximate=False)


def gather_layer(stacks, layer_index):
    (
        w_qkv,
        b_qv,
        w_out,
        b_out,
        gain_attn,
        shift_attn,
        w_up,
        b_up,
        w_down,
        b_down,
        gain_ffn,
        shift_ffn,
    ) = tuple((stacked[layer_index] for stacked in stacks))
    return (
        lax.all_gather(w_qkv, "fsdp", axis=0, tiled=True),
        lax.all_gather(b_qv, "fsdp", axis=0, tiled=True),
        lax.all_gather(w_out, "fsdp", axis=0, tiled=True),
        lax.all_gather(b_out, "fsdp", axis=0, tiled=True),
        lax.all_gather(gain_attn, "fsdp", axis=0, tiled=True),
        lax.all_gather(shift_attn, "fsdp", axis=0, tiled=True),
        lax.all_gather(w_up, "fsdp", axis=0, tiled=True),
        lax.all_gather(b_up, "fsdp", axis=0, tiled=True),
        lax.all_gather(w_down, "fsdp", axis=0, tiled=True),
        lax.all_gather(b_down, "fsdp", axis=0, tiled=True),
        lax.all_gather(gain_ffn, "fsdp", axis=0, tiled=True),
        lax.all_gather(shift_ffn, "fsdp", axis=0, tiled=True),
    )


def attend_forward(queries, keys_all, values_all, key_live):
    total_rows, local_heads = (queries.shape[0], queries.shape[1])
    block_rows = math.gcd(total_rows, 512)
    block_count = total_rows // block_rows
    score_scale = HD ** (-0.5)

    def one_block(query_block):
        scores = (
            jnp.einsum("qhd,khd->hqk", query_block, keys_all, preferred_element_type=jnp.float32)
            * score_scale
        )
        scores = jnp.where(key_live[None, None, :], scores, masked_score)
        top_score = jnp.max(scores, axis=-1, keepdims=True)
        exponent = jnp.exp(scores - top_score)
        row_total = jnp.sum(exponent, axis=-1, keepdims=True)
        probability = (exponent / row_total).astype(jnp.bfloat16)
        context = jnp.einsum(
            "hqk,khd->qhd", probability, values_all, preferred_element_type=jnp.float32
        )
        return (context.astype(jnp.bfloat16), (top_score + jnp.log(row_total))[..., 0])

    blocks = queries.reshape(block_count, block_rows, local_heads, HD)
    context, log_total = lax.map(one_block, blocks)
    return (context.reshape(total_rows, local_heads, HD), log_total)


def attend_backward(queries, keys_all, values_all, grad_context, log_total, key_live):
    total_rows, local_heads = (queries.shape[0], queries.shape[1])
    block_rows = math.gcd(total_rows, 512)
    block_count = total_rows // block_rows
    score_scale = HD ** (-0.5)

    def one_block(running, inputs):
        grad_keys, grad_values = running
        query_block, grad_block, log_block = inputs
        scores = (
            jnp.einsum("qhd,khd->hqk", query_block, keys_all, preferred_element_type=jnp.float32)
            * score_scale
        )
        scores = jnp.where(key_live[None, None, :], scores, masked_score)
        probability = jnp.exp(scores - log_block[:, :, None])
        grad_prob = jnp.einsum(
            "qhd,khd->hqk", grad_block, values_all, preferred_element_type=jnp.float32
        )
        grad_values = grad_values + jnp.einsum(
            "hqk,qhd->khd",
            probability.astype(jnp.bfloat16),
            grad_block,
            preferred_element_type=jnp.float32,
        )
        inner_sum = jnp.sum(grad_prob * probability, axis=-1, keepdims=True)
        grad_scores = (probability * (grad_prob - inner_sum)).astype(jnp.bfloat16)
        grad_query = (
            jnp.einsum("hqk,khd->qhd", grad_scores, keys_all, preferred_element_type=jnp.float32)
            * score_scale
        )
        grad_keys = (
            grad_keys
            + jnp.einsum(
                "hqk,qhd->khd", grad_scores, query_block, preferred_element_type=jnp.float32
            )
            * score_scale
        )
        return ((grad_keys, grad_values), grad_query)

    zero_keys = jnp.zeros((total_rows, local_heads, HD), jnp.float32)
    shaped = (
        queries.reshape(block_count, block_rows, local_heads, HD),
        grad_context.reshape(block_count, block_rows, local_heads, HD),
        log_total,
    )
    (grad_keys, grad_values), grad_queries = lax.scan(one_block, (zero_keys, zero_keys), shaped)
    return (grad_queries.reshape(total_rows, local_heads, HD), grad_keys, grad_values)


def layer_forward(hidden, weights, key_live):
    (
        w_qkv,
        b_qv,
        w_out,
        b_out,
        gain_attn,
        shift_attn,
        w_up,
        b_up,
        w_down,
        b_down,
        gain_ffn,
        shift_ffn,
    ) = weights
    local_rows = hidden.shape[0]
    groups = lax.axis_size("seq")
    local_heads = HEADS // groups
    bias_qv = b_qv.astype(jnp.float32)
    bias_full = jnp.concatenate([bias_qv[:D], jnp.zeros((D,), jnp.float32), bias_qv[D:]])
    hidden_low = hidden.astype(jnp.bfloat16)
    projected = (jnp.dot(hidden_low, w_qkv, preferred_element_type=jnp.float32) + bias_full).astype(
        jnp.bfloat16
    )
    by_head = lax.all_to_all(
        projected.reshape(local_rows, 3, groups, local_heads, HD),
        "seq",
        split_axis=2,
        concat_axis=0,
        tiled=True,
    )
    context, log_total = attend_forward(
        by_head[:, 0, 0], by_head[:, 1, 0], by_head[:, 2, 0], key_live
    )
    ctx_rows = lax.all_to_all(
        context.reshape(local_rows * groups, 1, local_heads, HD),
        "seq",
        split_axis=0,
        concat_axis=1,
        tiled=True,
    ).reshape(local_rows, D)
    attended = jnp.dot(ctx_rows, w_out, preferred_element_type=jnp.float32) + b_out.astype(
        jnp.float32
    )
    residual_one = hidden + attended
    normed = norm_rows(residual_one, gain_attn.astype(jnp.float32), shift_attn.astype(jnp.float32))
    pre_gelu = jnp.dot(
        normed.astype(jnp.bfloat16), w_up, preferred_element_type=jnp.float32
    ) + b_up.astype(jnp.float32)
    active = gelu_exact(pre_gelu).astype(jnp.bfloat16)
    branch_out = jnp.dot(active, w_down, preferred_element_type=jnp.float32) + b_down.astype(
        jnp.float32
    )
    residual_two = normed + branch_out
    output = norm_rows(residual_two, gain_ffn.astype(jnp.float32), shift_ffn.astype(jnp.float32))
    stored = (
        hidden,
        by_head,
        log_total,
        ctx_rows,
        residual_one,
        normed,
        pre_gelu,
        active,
        residual_two,
    )
    return (output, stored)


def layer_backward(grad_output, weights, stored, key_live):
    (
        w_qkv,
        b_qv,
        w_out,
        b_out,
        gain_attn,
        shift_attn,
        w_up,
        b_up,
        w_down,
        b_down,
        gain_ffn,
        shift_ffn,
    ) = weights
    hidden, by_head, log_total, ctx_rows, residual_one, normed, pre_gelu, active, residual_two = (
        stored
    )
    local_rows = hidden.shape[0]
    groups = lax.axis_size("seq")
    local_heads = HEADS // groups
    ffn_pull = jax.vjp(
        norm_rows, residual_two, gain_ffn.astype(jnp.float32), shift_ffn.astype(jnp.float32)
    )[1]
    grad_two, grad_gain_ffn, grad_shift_ffn = ffn_pull(grad_output)
    grad_branch = grad_two.astype(jnp.bfloat16)
    grad_b_down = jnp.sum(grad_branch.astype(jnp.float32), axis=0)
    grad_w_down = jnp.einsum("rf,rd->fd", active, grad_branch, preferred_element_type=jnp.float32)
    grad_active = jnp.einsum("rd,fd->rf", grad_branch, w_down, preferred_element_type=jnp.float32)
    gelu_pull = jax.vjp(gelu_exact, pre_gelu)[1]
    grad_pre = gelu_pull(grad_active)[0].astype(jnp.bfloat16)
    grad_b_up = jnp.sum(grad_pre.astype(jnp.float32), axis=0)
    normed_low = normed.astype(jnp.bfloat16)
    grad_w_up = jnp.einsum("rd,rf->df", normed_low, grad_pre, preferred_element_type=jnp.float32)
    grad_normed = (
        jnp.einsum("rf,df->rd", grad_pre, w_up, preferred_element_type=jnp.float32) + grad_two
    )
    attn_pull = jax.vjp(
        norm_rows, residual_one, gain_attn.astype(jnp.float32), shift_attn.astype(jnp.float32)
    )[1]
    grad_one, grad_gain_attn, grad_shift_attn = attn_pull(grad_normed)
    grad_attended = grad_one.astype(jnp.bfloat16)
    grad_b_out = jnp.sum(grad_attended.astype(jnp.float32), axis=0)
    grad_w_out = jnp.einsum(
        "rk,rd->kd", ctx_rows, grad_attended, preferred_element_type=jnp.float32
    )
    grad_ctx = jnp.einsum(
        "rd,kd->rk", grad_attended, w_out, preferred_element_type=jnp.float32
    ).astype(jnp.bfloat16)
    grad_heads = lax.all_to_all(
        grad_ctx.reshape(local_rows, groups, local_heads, HD),
        "seq",
        split_axis=1,
        concat_axis=0,
        tiled=True,
    )
    grad_queries, grad_keys, grad_values = attend_backward(
        by_head[:, 0, 0], by_head[:, 1, 0], by_head[:, 2, 0], grad_heads[:, 0], log_total, key_live
    )
    grad_stack = jnp.stack([grad_queries, grad_keys, grad_values], axis=1).astype(jnp.bfloat16)[
        :, :, None
    ]
    grad_projected = lax.all_to_all(
        grad_stack, "seq", split_axis=0, concat_axis=2, tiled=True
    ).reshape(local_rows, 3 * D)
    grad_sums = jnp.sum(grad_projected.astype(jnp.float32), axis=0)
    grad_b_qv = jnp.concatenate([grad_sums[:D], grad_sums[2 * D :]])
    hidden_low = hidden.astype(jnp.bfloat16)
    grad_w_qkv = jnp.einsum(
        "rd,re->de", hidden_low, grad_projected, preferred_element_type=jnp.float32
    )
    grad_hidden = (
        jnp.einsum("re,de->rd", grad_projected, w_qkv, preferred_element_type=jnp.float32)
        + grad_one
    )
    weight_grads = (
        grad_w_qkv,
        grad_b_qv,
        grad_w_out,
        grad_b_out,
        grad_gain_attn,
        grad_shift_attn,
        grad_w_up,
        grad_b_up,
        grad_w_down,
        grad_b_down,
        grad_gain_ffn,
        grad_shift_ffn,
    )
    return (grad_hidden, weight_grads)


def fsdp_layer_sum(weight_grads):
    (
        grad_w_qkv,
        grad_b_qv,
        grad_w_out,
        grad_b_out,
        grad_gain_attn,
        grad_shift_attn,
        grad_w_up,
        grad_b_up,
        grad_w_down,
        grad_b_down,
        grad_gain_ffn,
        grad_shift_ffn,
    ) = weight_grads
    return (
        lax.psum_scatter(grad_w_qkv, "fsdp", scatter_dimension=0, tiled=True),
        lax.psum_scatter(grad_b_qv, "fsdp", scatter_dimension=0, tiled=True),
        lax.psum_scatter(grad_w_out, "fsdp", scatter_dimension=0, tiled=True),
        lax.psum_scatter(grad_b_out, "fsdp", scatter_dimension=0, tiled=True),
        lax.psum_scatter(grad_gain_attn, "fsdp", scatter_dimension=0, tiled=True),
        lax.psum_scatter(grad_shift_attn, "fsdp", scatter_dimension=0, tiled=True),
        lax.psum_scatter(grad_w_up, "fsdp", scatter_dimension=0, tiled=True),
        lax.psum_scatter(grad_b_up, "fsdp", scatter_dimension=0, tiled=True),
        lax.psum_scatter(grad_w_down, "fsdp", scatter_dimension=0, tiled=True),
        lax.psum_scatter(grad_b_down, "fsdp", scatter_dimension=0, tiled=True),
        lax.psum_scatter(grad_gain_ffn, "fsdp", scatter_dimension=0, tiled=True),
        lax.psum_scatter(grad_shift_ffn, "fsdp", scatter_dimension=0, tiled=True),
    )


def seq_total_sum(shard_grads, grad_memory):
    (
        grad_w_qkv,
        grad_b_qv,
        grad_w_out,
        grad_b_out,
        grad_gain_attn,
        grad_shift_attn,
        grad_w_up,
        grad_b_up,
        grad_w_down,
        grad_b_down,
        grad_gain_ffn,
        grad_shift_ffn,
    ) = shard_grads
    pieces = (
        lax.psum_scatter(
            grad_w_qkv.astype(jnp.bfloat16), "seq", scatter_dimension=2, tiled=True
        ).astype(jnp.float32),
        lax.psum_scatter(
            grad_w_out.astype(jnp.bfloat16), "seq", scatter_dimension=2, tiled=True
        ).astype(jnp.float32),
        lax.psum_scatter(
            grad_w_up.astype(jnp.bfloat16), "seq", scatter_dimension=2, tiled=True
        ).astype(jnp.float32),
        lax.psum_scatter(
            grad_w_down.astype(jnp.bfloat16), "seq", scatter_dimension=2, tiled=True
        ).astype(jnp.float32),
    )
    matrices = (
        lax.all_gather(pieces[0].astype(jnp.bfloat16), "seq", axis=2, tiled=True).astype(
            jnp.float32
        ),
        lax.all_gather(pieces[1].astype(jnp.bfloat16), "seq", axis=2, tiled=True).astype(
            jnp.float32
        ),
        lax.all_gather(pieces[2].astype(jnp.bfloat16), "seq", axis=2, tiled=True).astype(
            jnp.float32
        ),
        lax.all_gather(pieces[3].astype(jnp.bfloat16), "seq", axis=2, tiled=True).astype(
            jnp.float32
        ),
    )
    smalls = (
        lax.psum(grad_b_qv.astype(jnp.bfloat16), "seq").astype(jnp.float32),
        lax.psum(grad_b_out.astype(jnp.bfloat16), "seq").astype(jnp.float32),
        lax.psum(grad_gain_attn.astype(jnp.bfloat16), "seq").astype(jnp.float32),
        lax.psum(grad_shift_attn.astype(jnp.bfloat16), "seq").astype(jnp.float32),
        lax.psum(grad_b_up.astype(jnp.bfloat16), "seq").astype(jnp.float32),
        lax.psum(grad_b_down.astype(jnp.bfloat16), "seq").astype(jnp.float32),
        lax.psum(grad_gain_ffn.astype(jnp.bfloat16), "seq").astype(jnp.float32),
        lax.psum(grad_shift_ffn.astype(jnp.bfloat16), "seq").astype(jnp.float32),
        lax.psum(grad_memory.astype(jnp.bfloat16), "seq").astype(jnp.float32),
    )
    weights_sum = (
        matrices[0],
        smalls[0],
        matrices[1],
        smalls[1],
        smalls[2],
        smalls[3],
        matrices[2],
        smalls[4],
        matrices[3],
        smalls[5],
        smalls[6],
        smalls[7],
    )
    return (weights_sum, smalls[8])


def body(
    tokens,
    memory,
    lengths,
    w_qkv,
    b_qv,
    w_out,
    b_out,
    gain_attn,
    shift_attn,
    w_up,
    b_up,
    w_down,
    b_down,
    gain_ffn,
    shift_ffn,
    cotangent,
):
    local_rows = tokens.shape[0]
    groups = lax.axis_size("seq")
    seq_place = lax.axis_index("seq")
    length = lengths[0]
    positions = seq_place * local_rows + jnp.arange(local_rows, dtype=jnp.int32)
    key_live = jnp.arange(local_rows * groups, dtype=jnp.int32) < length + 2 * MEM
    row_live = (positions < length + 2 * MEM)[:, None]
    token_live = ((positions >= MEM) & (positions < length + MEM))[:, None]
    memory_slots = jnp.arange(2 * MEM, dtype=jnp.int32)
    targets = jnp.where(memory_slots < MEM, memory_slots, length + memory_slots)
    select = positions[:, None] == targets[None, :]
    hidden = jnp.where(token_live, tokens.astype(jnp.float32), 0.0) + jnp.dot(
        select.astype(jnp.bfloat16), memory[0], preferred_element_type=jnp.float32
    )
    stacks = (
        w_qkv,
        b_qv,
        w_out,
        b_out,
        gain_attn,
        shift_attn,
        w_up,
        b_up,
        w_down,
        b_down,
        gain_ffn,
        shift_ffn,
    )
    layer_inputs = []
    for layer_index in range(LAYERS):
        weights = gather_layer(stacks, layer_index)
        layer_inputs.append(hidden)
        hidden, stored = layer_forward(hidden, weights, key_live)
    result = jnp.where(row_live, hidden, 0.0)
    grad_hidden = jnp.where(row_live, cotangent, 0.0)
    collected = []
    for layer_index in reversed(range(LAYERS)):
        weights = gather_layer(stacks, layer_index)
        stored = layer_forward(layer_inputs[layer_index], weights, key_live)[1]
        grad_hidden, weight_grads = layer_backward(grad_hidden, weights, stored, key_live)
        collected.insert(0, fsdp_layer_sum(weight_grads))
    stacked_grads = tuple((jnp.stack(member) for member in zip(*collected)))
    grad_tokens = jnp.where(token_live, grad_hidden, 0.0)
    grad_memory = jnp.dot(
        select.astype(jnp.float32).T, grad_hidden, precision=lax.Precision.HIGHEST
    )[None]
    summed, memory_sum = seq_total_sum(stacked_grads, grad_memory)
    return (result, grad_tokens, memory_sum) + tuple(summed)


def solution(mesh):
    in_specs = (
        P(("fsdp", "seq"), None),
        P("fsdp", None, None),
        P("fsdp"),
        P(None, "fsdp", None),
        P(None, "fsdp"),
        P(None, "fsdp", None),
        P(None, "fsdp"),
        P(None, "fsdp"),
        P(None, "fsdp"),
        P(None, "fsdp", None),
        P(None, "fsdp"),
        P(None, "fsdp", None),
        P(None, "fsdp"),
        P(None, "fsdp"),
        P(None, "fsdp"),
        P(("fsdp", "seq"), None),
    )
    out_specs = (
        P(("fsdp", "seq"), None),
        P(("fsdp", "seq"), None),
        P("fsdp", None, None),
        P(None, "fsdp", None),
        P(None, "fsdp"),
        P(None, "fsdp", None),
        P(None, "fsdp"),
        P(None, "fsdp"),
        P(None, "fsdp"),
        P(None, "fsdp", None),
        P(None, "fsdp"),
        P(None, "fsdp", None),
        P(None, "fsdp"),
        P(None, "fsdp"),
        P(None, "fsdp"),
    )
    return jax.shard_map(body, mesh=mesh, in_specs=in_specs, out_specs=out_specs, check_vma=False)
```

profile of v0, /device:TPU:0, one launch (start us, length us, event | category | flops | bytes accessed | tf_op | source)
XLA Modules:
  0.0 1167.0 jit_solution(7065298566973791813)
XLA Ops:
  20.1 26.5 %all-reduce.32 = (bf16[1536]{0:T(1024)(128)(2,1)S(1)}, bf16[768]{0:T(1024)(128)(2,1)S(1)}, bf16[768]{0:T(1024)(128)(2,1)S(1)}, bf16[768]{0:T(1024)(128)(2,1)S(1)...) all-reduce(bf16[1536]{0:T(1024)(128)(2,1)S(1)} %dynamic-update-slic, ...), channel_id=3, replica_groups=mesh['fsdp'=8,'seq'=4] {'fsdp'}, use_global_device_ids=true, to_apply=%add | all-reduce | flops 12288 | bytes 49152
  56.3 4.9 all-to-all-start
  63.6 7.9 all-gather.7
  72.2 15.6 %all-to-all-done = bf16[256,3,4,3,64]{0,4,3,1,2:T(8,128)(2,1)S(1)} async-done(((bf16[256,3,4,3,64]{0,4,3,1,2:T(8,128)(2,1)}), bf16[256,3,4,3,64]{0,4,3,1,2:T(8,128)(2,1)S(1)}, u32[]{:S(2)}, u32[]{:S(2)}) %all-to-all-start) | async-done | bytes 1179680 | tf_op jit(solution)/shard_map/all_to_all | solution.py:160
  88.4 17.2 %while.78 = (s32[]{:T(128)}, bf16[2,512,3,64]{1,3,2,0:T(8,128)(2,1)S(1)}, bf16[2,512,3,64]{1,3,2,0:T(8,128)(2,1)S(1)}, bf16[1024,3,64]{0,2,1:T(8,128)(2,1)S(1)},...) while((s32[]{:T(128)}, bf16[2,512,3,64]{1,3,2,0:T(8,128)(2,1)S(1)}, ...), condition=%wide.region_3.4_spmd.clone, body=%wide.region_0.3_spmd.clone.sunk | while | flops 412190720 | bytes 13779033 | solution.py:83
  111.4 9.5 while.80
  126.3 5.1 all-to-all-start.4
  137.5 18.7 %all-gather.45.cloned.1.call-done = bf16[1,3072,768]{2,1,0:T(8,128)(2,1)} async-done(((bf16[1,384,768]{2,1,0:T(8,128)(2,1)}), bf16[1,3072,768]{2,1,0:T(8,128)(2,1)}) %all-gather.45.cloned.1.call-update) | async-done | bytes 4718608 | tf_op jit(solution)/shard_map/all_gather | solution.py:54
  156.1 13.0 %fusion.515 = (f32[256]{0:T(256)S(1)}, f32[256,768]{1,0:T(8,128)S(1)}) fusion(f32[768]{0:T(1024)} %convert_element_type.372, bf16[1,3072,768]{2,1,0:T(8,128)(2,1)} %all-gather.45.cloned.1.call-done, bf16[1,768,3072]{2,1,0:T(8,128)(2,1)} %all-gather.43.cloned.1.call-done, f32[3072]{0:T(1024)} %bitcast.592, f32[256,768]{1,0:T(8,128)S(1)} %get-tuple-element.950, ...), kind=kOutput, calls=%fused_computation.609 | convolution fusion | flops 2470182656 | bytes 11034624 | tf_op jit(solution)/shard_map/dot_general | solution.py:186
  169.4 23.0 %all-gather.47.cloned.1.call-done = bf16[1,768,2304]{2,1,0:T(8,128)(2,1)} async-done(((bf16[1,96,2304]{2,1,0:T(8,128)(2,1)}), bf16[1,768,2304]{2,1,0:T(8,128)(2,1)}) %all-gather.47.cloned.1.call-update) | async-done | bytes 3538960 | tf_op jit(solution)/shard_map/all_gather | solution.py:46
  206.1 8.8 all-gather.19
  223.2 10.1 all-to-all-done.2
  235.2 17.3 %while.79 = (s32[]{:T(128)}, bf16[2,512,3,64]{1,3,2,0:T(8,128)(2,1)S(1)}, bf16[2,512,3,64]{1,3,2,0:T(8,128)(2,1)S(1)}, bf16[1024,3,64]{0,2,1:T(8,128)(2,1)S(1)},...) while((s32[]{:T(128)}, bf16[2,512,3,64]{1,3,2,0:T(8,128)(2,1)S(1)}, ...), condition=%wide.region_11.12_spmd.clone, body=%wide.region_8.11_spmd.clone.sunk | while | flops 412190720 | bytes 13779033 | solution.py:83
  258.1 9.5 while.81
  269.8 5.1 all-to-all-start.5
  279.5 21.1 %all-gather.53.cloned.1.call-done = bf16[1,3072,768]{2,1,0:T(8,128)(2,1)} async-done(((bf16[1,384,768]{2,1,0:T(8,128)(2,1)}), bf16[1,3072,768]{2,1,0:T(8,128)(2,1)}) %all-gather.53.cloned.1.call-update) | async-done | bytes 4718608 | tf_op jit(solution)/shard_map/all_gather | solution.py:54
  300.6 13.6 %fusion.523 = (f32[256]{0:T(256)}, f32[256,768]{1,0:T(8,128)S(1)}) fusion(f32[768]{0:T(1024)} %convert_element_type.379, bf16[1,3072,768]{2,1,0:T(8,128)(2,1)} %all-gather.53.cloned.1.call-done, bf16[1,768,3072]{2,1,0:T(8,128)(2,1)} %all-gather.51.cloned.1.call-done, f32[3072]{0:T(1024)} %bitcast.594, f32[256,768]{1,0:T(8,128)S(1)} %get-tuple-element.959, ...), kind=kOutput, calls=%fused_computation.613 | convolution fusion | flops 2470182656 | bytes 11034624 | tf_op jit(solution)/shard_map/dot_general | solution.py:186
  321.0 11.1 multiply_convert_fusion.3
  338.0 5.1 fusion.533
  343.2 6.9 convert_reduce_fusion
  350.1 6.2 multiply_reduce_fusion.4
  359.4 5.1 all-to-all-start.6
  365.4 11.2 all-to-all-done.6
  378.1 27.1 %while.82 = (s32[]{:T(128)}, f32[1024,3,64]{0,2,1:T(8,128)}, f32[1024,3,64]{0,2,1:T(8,128)}, bf16[2,512,3,64]{1,3,2,0:T(8,128)(2,1)}, bf16[2,512,3,64]{1,3,2,0:T...) while((s32[]{:T(128)}, f32[1024,3,64]{0,2,1:T(8,128)}, ...), condition=%wide.region_36.37_spmd.clone, body=%wide.region_34.36_spmd.clone.sunk | while | flops 1031306752 | bytes 112560032 | solution.py:132
  421.5 12.5 %multiply_convert_fusion.2 = (bf16[256,3072]{1,0:T(8,128)(2,1)S(1)}, f32[256,3072]{1,0:T(8,128)}, f32[256,3072]{1,0:T(8,128)}) fusion(f32[3072]{0:T(1024)S(1)} %bitcast.593, bf16[1,768,3072]{2,1,0:T(8,128)(2,1)} %all-gather.43.cloned.1.call-done, f32[256,768]{1,0:T(8,128)} %get-tuple-element.963, f32[768]{0:T(1024)S(1)} %copy-done.72, ...), kind=kOutput, calls=%fused_computation.203 | convolution fusion | flops 1260847104 | bytes 13389824 | tf_op jit(solution)/shard_map/dot_general | solution.py:182
  439.5 10.0 all-to-all-done.7
  464.3 5.0 fusion.532
  470.5 7.7 fusion.484
  478.4 8.8 convert_reduce_fusion.1
  488.4 5.3 fusion.487
  497.0 5.1 multiply_reduce_fusion.5
  516.7 11.5 all-to-all-done.8
  529.6 29.8 %while.83 = (s32[]{:T(128)}, f32[1024,3,64]{0,2,1:T(8,128)}, f32[1024,3,64]{0,2,1:T(8,128)}, bf16[2,512,3,64]{1,3,2,0:T(8,128)(2,1)}, bf16[2,512,3,64]{1,3,2,0:T...) while((s32[]{:T(128)}, f32[1024,3,64]{0,2,1:T(8,128)}, ...), condition=%wide.region_45.46_spmd.clone, body=%wide.region_43.45_spmd.clone.sunk | while | flops 1031306752 | bytes 107792680 | solution.py:132
  571.5 31.3 %all_to_all.166 = bf16[4,2,73728]{2,1,0:T(2,128)(2,1)S(1)} all-to-all(bf16[4,2,73728]{2,1,0:T(2,128)(2,1)} %reshape.628), channel_id=1, replica_groups=mesh['fsdp'=8,'seq'=4] {'seq'}, dimensions={0} | all-to-all | bytes 2359296 | tf_op jit(solution)/shard_map/all_to_all | solution.py:267
  606.1 4.8 copy.238
  625.5 78.5 %reduce-scatter.24.cloned.1.call-done = f32[96,3072]{1,0:T(8,128)} async-done(((f32[768,3072]{1,0:T(8,128)}), f32[96,3072]{1,0:T(8,128)}) %reduce-scatter.24.cloned.1.call-update) | async-done | bytes 1179664 | tf_op jit(solution)/shard_map/reduce_scatter | solution.py:319
  706.9 43.6 %reduce-scatter.22.cloned.1.call-done = f32[96,768]{1,0:T(8,128)} async-done(((f32[768,768]{1,0:T(8,128)}), f32[96,768]{1,0:T(8,128)}) %reduce-scatter.22.cloned.1.call-update) | async-done | bytes 294928 | tf_op jit(solution)/shard_map/reduce_scatter | solution.py:315
  751.4 45.7 %reduce-scatter.20.cloned.1.call-done = f32[96,768]{1,0:T(8,128)} async-done(((f32[768,768]{1,0:T(8,128)}), f32[96,768]{1,0:T(8,128)}) %reduce-scatter.20.cloned.1.call-update) | async-done | bytes 294928 | tf_op jit(solution)/shard_map/reduce_scatter | solution.py:315
  799.6 66.4 %reduce-scatter.18.cloned.1.call-done = f32[96,2304]{1,0:T(8,128)} async-done(((f32[768,2304]{1,0:T(8,128)}), f32[96,2304]{1,0:T(8,128)}) %reduce-scatter.18.cloned.1.call-update) | async-done | bytes 884752 | tf_op jit(solution)/shard_map/reduce_scatter | solution.py:313
  867.2 68.1 %reduce-scatter.16.cloned.1.call-done = f32[96,2304]{1,0:T(8,128)} async-done(((f32[768,2304]{1,0:T(8,128)}), f32[96,2304]{1,0:T(8,128)}) %reduce-scatter.16.cloned.1.call-update) | async-done | bytes 884752 | tf_op jit(solution)/shard_map/reduce_scatter | solution.py:313
  951.2 42.3 %all-reduce.36.cloned.1.call-done = bf16[2,384,768]{1,0,2:T(2,128)(2,1)} async-done(((bf16[2,384,768]{1,0,2:T(2,128)(2,1)}), bf16[2,384,768]{1,0,2:T(2,128)(2,1)}) %all-reduce.36.cloned.1.call-update) | async-done | bytes 1179664
  995.9 26.1 %all-reduce.31 = (bf16[1536]{0:T(1024)(128)(2,1)S(1)}, bf16[1536]{0:T(1024)(128)(2,1)S(1)}, bf16[768]{0:T(1024)(128)(2,1)S(1)}, bf16[768]{0:T(1024)(128)(2,1)S(1...) all-reduce(f32[1536]{0:T(1024)S(1)} %pad_maximum_fusion.9, ...), channel_id=30, replica_groups=mesh['fsdp'=8,'seq'=4] {'fsdp'}, use_global_device_ids=true, to_apply=%region_53.54.clone | all-reduce | flops 18432 | bytes 110592
  1029.4 18.0 %all-reduce.33 = (bf16[1,20,768]{2,1,0:T(8,128)(2,1)S(1)}, bf16[2,192]{1,0:T(2,128)(2,1)S(1)}, bf16[2,96]{1,0:T(2,128)(2,1)S(1)}, bf16[2,96]{1,0:T(2,128)(2,1)S(...) all-reduce(bf16[1,20,768]{2,1,0:T(8,128)(2,1)S(1)} %fusion.366, ...), channel_id=1, replica_groups=mesh['fsdp'=8,'seq'=4] {'seq'}, use_global_device_ids=true, to_apply=%region_46.47 | all-reduce | flops 17664 | bytes 70656 | tf_op jit(solution)/shard_map/psum | solution.py:380
  1053.7 17.7 %all_gather.131 = bf16[2,96,768]{1,0,2:T(2,128)(2,1)S(1)} all-gather(bf16[2,96,192]{1,0,2:T(2,128)(2,1)S(1)} %bitcast.591), channel_id=1, replica_groups=mesh['fsdp'=8,'seq'=4] {'seq'}, dimensions={2}, use_global_device_ids=true | all-gather | bytes 368640 | tf_op jit(solution)/shard_map/all_gather | solution.py:361
  1072.4 9.5 reduce-scatter.34.cloned.1.call-done
  1083.0 35.1 %all_gather.130 = bf16[2,96,2304]{1,0,2:T(2,128)(2,1)S(1)} all-gather(bf16[2,96,576]{1,0,2:T(2,128)(2,1)S(1)} %bitcast.589), channel_id=1, replica_groups=mesh['fsdp'=8,'seq'=4] {'seq'}, dimensions={2}, use_global_device_ids=true | all-gather | bytes 1105920 | tf_op jit(solution)/shard_map/all_gather | solution.py:358
  1124.5 5.1 copy.228
  1129.5 27.2 %all-gather.35.cloned.1.call-done = bf16[2,96,3072]{2,1,0:T(8,128)(2,1)} async-done(((bf16[2,96,768]{2,1,0:T(8,128)(2,1)}), bf16[2,96,3072]{2,1,0:T(8,128)(2,1)}) %all-gather.35.cloned.1.call-update) | async-done | bytes 1179664 | tf_op jit(solution)/shard_map/all_gather | solution.py:364
  (724 shorter events, 340.6 us)
Async XLA Ops:
  7.2 42.3 %all-gather.39.cloned.1.call-start = ((), (), s32[]{:S(2)}) async-start(), calls=%async_computation.32 | async-start | bytes 3981312 | tf_op jit(solution)/shard_map/all_gather | solution.py:46
  9.6 125.8 %all-gather.41.cloned.1.call-start = ((), (), s32[]{:S(2)}) async-start(), calls=%async_computation.33 | async-start | bytes 1327104 | tf_op jit(solution)/shard_map/all_gather | solution.py:48
  11.5 126.0 %all-gather.43.cloned.1.call-start = ((), (), s32[]{:S(2)}) async-start(), calls=%async_computation.34 | async-start | bytes 5308416 | tf_op jit(solution)/shard_map/all_gather | solution.py:52
  12.6 143.5 %all-gather.45.cloned.1.call-start = ((), (), s32[]{:S(2)}) async-start(), calls=%async_computation.35 | async-start | bytes 5308416 | tf_op jit(solution)/shard_map/all_gather | solution.py:54
  13.9 178.6 %all-gather.47.cloned.1.call-start = ((), (), s32[]{:S(2)}) async-start(), calls=%async_computation.36 | async-start | bytes 3981312 | tf_op jit(solution)/shard_map/all_gather | solution.py:46
  14.4 262.3 %all-gather.49.cloned.1.call-start = ((), (), s32[]{:S(2)}) async-start(), calls=%async_computation.37 | async-start | bytes 1327104 | tf_op jit(solution)/shard_map/all_gather | solution.py:48
  48.7 171.8 %copy-start.13 = (f32[256,768]{1,0:T(8,128)}, f32[256,768]{1,0:T(8,128)S(1)}, u32[]{:S(2)}) copy-start(f32[256,768]{1,0:T(8,128)S(1)} %convolution_add_fusion.2) | copy-start | bytes 2359300
  56.3 31.5 %all-to-all-start = ((bf16[256,3,4,3,64]{0,4,3,1,2:T(8,128)(2,1)}), bf16[256,3,4,3,64]{0,4,3,1,2:T(8,128)(2,1)S(1)}, u32[]{:S(2)}, u32[]{:S(2)}) async-start(bf16[256,3,4,3,64]{0,4,3,1,2:T(8,128)(2,1)} %copy.177), calls=%async_computation | async-start | bytes 2359296 | tf_op jit(solution)/shard_map/all_to_all | solution.py:160
  61.1 218.3 %all-gather.51.cloned.1.call-start = ((), (), s32[]{:S(2)}) async-start(), calls=%async_computation.38 | async-start | bytes 5308416 | tf_op jit(solution)/shard_map/all_gather | solution.py:52
  62.5 93.7 %copy-start.67 = (f32[768]{0:T(1024)}, f32[768]{0:T(1024)S(1)}, u32[]{:S(2)}) copy-start(f32[768]{0:T(1024)S(1)} %convert_element_type.370) | copy-start | bytes 9220
  62.5 93.7 %copy-start.71 = (f32[768]{0:T(1024)}, f32[768]{0:T(1024)S(1)}, u32[]{:S(2)}) copy-start(f32[768]{0:T(1024)S(1)} %convert_element_type.371) | copy-start | bytes 9220
  72.2 246.0 %copy-start.65 = (f32[768]{0:T(1024)}, f32[768]{0:T(1024)S(1)}, u32[]{:S(2)}) copy-start(f32[768]{0:T(1024)S(1)} %convert_element_type.373) | copy-start | bytes 9220
  72.2 246.0 %copy-start.69 = (f32[768]{0:T(1024)}, f32[768]{0:T(1024)S(1)}, u32[]{:S(2)}) copy-start(f32[768]{0:T(1024)S(1)} %convert_element_type.374) | copy-start | bytes 9220
  107.7 17.8 %all-to-all-start.1 = ((bf16[4,2,24576]{2,1,0:T(2,128)(2,1)}), bf16[4,2,24576]{2,1,0:T(2,128)(2,1)S(1)}, u32[]{:S(2)}, u32[]{:S(2)}) async-start(bf16[4,2,24576]{2,1,0:T(2,128)(2,1)} %reshape.622), calls=%async_computation.1 | async-start | bytes 786432 | tf_op jit(solution)/shard_map/all_to_all | solution.py:170
  126.3 73.1 %all-to-all-start.4 = ((bf16[4,2,24576]{2,1,0:T(2,128)(2,1)}), bf16[4,2,24576]{2,1,0:T(2,128)(2,1)S(1)}, u32[]{:S(2)}, u32[]{:S(2)}) async-start(bf16[4,2,24576]{2,1,0:T(2,128)(2,1)} %reshape.620), calls=%async_computation.4 | async-start | bytes 786432 | tf_op jit(solution)/shard_map/all_to_all | solution.py:170
  199.4 34.0 %all-to-all-start.2 = ((bf16[256,3,4,3,64]{0,4,3,1,2:T(8,128)(2,1)}), bf16[256,3,4,3,64]{0,4,3,1,2:T(8,128)(2,1)}, u32[]{:S(2)}, u32[]{:S(2)}) async-start(bf16[256,3,4,3,64]{0,4,3,1,2:T(8,128)(2,1)} %copy.185), calls=%async_computation.2 | async-start | bytes 2359296 | tf_op jit(solution)/shard_map/all_to_all | solution.py:160
  204.1 96.4 %all-gather.53.cloned.1.call-start = ((), (), s32[]{:S(2)}) async-start(), calls=%async_computation.39 | async-start | bytes 5308416 | tf_op jit(solution)/shard_map/all_gather | solution.py:54
  205.5 126.6 %copy-start.73 = (f32[768]{0:T(1024)}, f32[768]{0:T(1024)S(1)}, u32[]{:S(2)}) copy-start(f32[768]{0:T(1024)S(1)} %convert_element_type.378) | copy-start | bytes 9220
  254.6 15.2 %all-to-all-start.3 = ((bf16[4,2,24576]{2,1,0:T(2,128)(2,1)}), bf16[4,2,24576]{2,1,0:T(2,128)(2,1)S(1)}, u32[]{:S(2)}, u32[]{:S(2)}) async-start(bf16[4,2,24576]{2,1,0:T(2,128)(2,1)} %reshape.630), calls=%async_computation.3 | async-start | bytes 786432 | tf_op jit(solution)/shard_map/all_to_all | solution.py:170
  269.8 45.8 %all-to-all-start.5 = ((bf16[4,2,24576]{2,1,0:T(2,128)(2,1)}), bf16[4,2,24576]{2,1,0:T(2,128)(2,1)}, u32[]{:S(2)}, u32[]{:S(2)}) async-start(bf16[4,2,24576]{2,1,0:T(2,128)(2,1)} %reshape.624), calls=%async_computation.5 | async-start | bytes 786432 | tf_op jit(solution)/shard_map/all_to_all | solution.py:170
  274.9 340.4 %reduce-scatter.32.cloned.1.call-start = ((), (), s32[]{:S(2)}) async-start(), calls=%async_computation.30 | async-start | bytes 10616832 | tf_op jit(solution)/shard_map/reduce_scatter | solution.py:321
  359.4 17.2 %all-to-all-start.6 = ((bf16[256,4,3,64]{0,3,2,1:T(8,128)(2,1)}), bf16[256,4,3,64]{0,3,2,1:T(8,128)(2,1)S(1)}, u32[]{:S(2)}, u32[]{:S(2)}) async-start(bf16[256,4,3,64]{0,3,2,1:T(8,128)(2,1)} %bitcast.582), calls=%async_computation.6 | async-start | bytes 786432 | tf_op jit(solution)/shard_map/all_to_all | solution.py:254
  417.0 32.5 %all-to-all-start.7 = ((bf16[4,2,73728]{2,1,0:T(2,128)(2,1)}), bf16[4,2,73728]{2,1,0:T(2,128)(2,1)}, u32[]{:S(2)}, u32[]{:S(2)}) async-start(bf16[4,2,73728]{2,1,0:T(2,128)(2,1)} %reshape.626), calls=%async_computation.7 | async-start | bytes 2359296 | tf_op jit(solution)/shard_map/all_to_all | solution.py:267
  421.4 195.2 %reduce-scatter.30.cloned.1.call-start = ((), (), s32[]{:S(2)}) async-start(), calls=%async_computation.29 | async-start | bytes 10616832 | tf_op jit(solution)/shard_map/reduce_scatter | solution.py:321
  469.4 154.8 %reduce-scatter.26.cloned.1.call-start = ((), (), s32[]{:S(2)}) async-start(), calls=%async_computation.26 | async-start | bytes 10616832 | tf_op jit(solution)/shard_map/reduce_scatter | solution.py:319
  478.2 225.8 %reduce-scatter.24.cloned.1.call-start = ((), (), s32[]{:S(2)}) async-start(), calls=%async_computation.25 | async-start | bytes 10616832 | tf_op jit(solution)/shard_map/reduce_scatter | solution.py:319
  493.7 256.7 %reduce-scatter.22.cloned.1.call-start = ((), (), s32[]{:S(2)}) async-start(), calls=%async_computation.24 | async-start | bytes 2654208 | tf_op jit(solution)/shard_map/reduce_scatter | solution.py:315
  496.9 300.2 %reduce-scatter.20.cloned.1.call-start = ((), (), s32[]{:S(2)}) async-start(), calls=%async_computation.23 | async-start | bytes 2654208 | tf_op jit(solution)/shard_map/reduce_scatter | solution.py:315
  506.0 360.0 %reduce-scatter.18.cloned.1.call-start = ((), (), s32[]{:S(2)}) async-start(), calls=%async_computation.22 | async-start | bytes 7962624 | tf_op jit(solution)/shard_map/reduce_scatter | solution.py:313
  512.9 15.3 %all-to-all-start.8 = ((bf16[256,4,3,64]{0,3,2,1:T(8,128)(2,1)}), bf16[256,4,3,64]{0,3,2,1:T(8,128)(2,1)S(1)}, u32[]{:S(2)}, u32[]{:S(2)}) async-start(bf16[256,4,3,64]{0,3,2,1:T(8,128)(2,1)} %bitcast.60), calls=%async_computation.8 | async-start | bytes 786432 | tf_op jit(solution)/shard_map/all_to_all | solution.py:254
  516.4 418.9 %reduce-scatter.16.cloned.1.call-start = ((), (), s32[]{:S(2)}) async-start(), calls=%async_computation.21 | async-start | bytes 7962624 | tf_op jit(solution)/shard_map/reduce_scatter | solution.py:313
  615.2 378.3 %all-reduce.36.cloned.1.call-start = ((), (), s32[]{:S(2)}) async-start(), calls=%async_computation.42 | async-start | bytes 2359296
  620.9 403.5 %reduce-scatter.28.cloned.1.call-start = ((), (), s32[]{:S(2)}) async-start(), calls=%async_computation.27 | async-start | bytes 1474560 | tf_op jit(solution)/shard_map/reduce_scatter | solution.py:350
  706.6 346.1 %reduce-scatter.36.cloned.1.call-start = ((), (), s32[]{:S(2)}) async-start(), calls=%async_computation.41 | async-start | bytes 491520
  799.5 282.3 %reduce-scatter.34.cloned.1.call-start = ((), (), s32[]{:S(2)}) async-start(), calls=%async_computation.40 | async-start | bytes 1474560
  945.0 50.9 %copy-start.85 = (f32[768]{0:T(1024)S(1)}, f32[768]{0:T(1024)}, u32[]{:S(2)}) copy-start(f32[768]{0:T(1024)} %get-tuple-element.880) | copy-start | bytes 9220
  945.0 50.9 %copy-start.86 = (f32[768]{0:T(1024)S(1)}, f32[768]{0:T(1024)}, u32[]{:S(2)}) copy-start(f32[768]{0:T(1024)} %get-tuple-element.884) | copy-start | bytes 9220
  945.0 50.9 %copy-start.100 = (f32[3072]{0:T(1024)S(1)}, f32[3072]{0:T(1024)}, u32[]{:S(2)}) copy-start(f32[3072]{0:T(1024)} %get-tuple-element.972) | copy-start | bytes 36868
  945.0 50.9 %copy-start.101 = (f32[3072]{0:T(1024)S(1)}, f32[3072]{0:T(1024)}, u32[]{:S(2)}) copy-start(f32[3072]{0:T(1024)} %get-tuple-element.974) | copy-start | bytes 36868
  945.0 50.9 %copy-start.117 = (f32[768]{0:T(1024)S(1)}, f32[768]{0:T(1024)}, u32[]{:S(2)}) copy-start(f32[768]{0:T(1024)} %get-tuple-element.737) | copy-start | bytes 9220
  945.0 50.9 %copy-start.118 = (f32[768]{0:T(1024)S(1)}, f32[768]{0:T(1024)}, u32[]{:S(2)}) copy-start(f32[768]{0:T(1024)} %get-tuple-element.742) | copy-start | bytes 9220
  945.0 50.9 %copy-start.119 = (f32[768]{0:T(1024)S(1)}, f32[768]{0:T(1024)}, u32[]{:S(2)}) copy-start(f32[768]{0:T(1024)} %get-tuple-element.733) | copy-start | bytes 9220
  945.1 50.9 %copy-start.120 = (f32[768]{0:T(1024)S(1)}, f32[768]{0:T(1024)}, u32[]{:S(2)}) copy-start(f32[768]{0:T(1024)} %get-tuple-element.740) | copy-start | bytes 9220
  945.1 50.9 %copy-start.121 = (f32[768]{0:T(1024)S(1)}, f32[768]{0:T(1024)}, u32[]{:S(2)}) copy-start(f32[768]{0:T(1024)} %get-tuple-element.735) | copy-start | bytes 9220
  945.1 79.8 %copy-start.28 = (f32[256,768]{1,0:T(8,128)S(1)}, f32[256,768]{1,0:T(8,128)}, u32[]{:S(2)}) copy-start(f32[256,768]{1,0:T(8,128)} %copy-done.27) | copy-start | bytes 2359300
  945.1 79.8 %copy-start.96 = (pred[256]{0:T(512)(128)(4,1)S(1)}, pred[256]{0:T(512)(128)(4,1)}, u32[]{:S(2)}) copy-start(pred[256]{0:T(512)(128)(4,1)} %copy-done.95) | copy-start | bytes 772
  945.1 179.3 %all-gather.37.cloned.1.call-start = ((), (), s32[]{:S(2)}) async-start(), calls=%async_computation.31 | async-start | bytes 1474560 | tf_op jit(solution)/shard_map/all_gather | solution.py:367
  995.4 161.4 %all-gather.35.cloned.1.call-start = ((), (), s32[]{:S(2)}) async-start(), calls=%async_computation.28 | async-start | bytes 1474560 | tf_op jit(solution)/shard_map/all_gather | solution.py:364
  (146 other events, 1343.9 us)
Sparse Core Ops, SparseCore 0:
  10.5 36.8 all-gather.38
  49.3 24.1 all-gather.40
  75.9 38.9 all-gather.42
  117.2 38.9 all-gather.44
  158.4 33.9 all-gather.46
  194.2 24.0 all-gather.48
  220.8 38.9 all-gather.50
  261.6 38.8 all-gather.52
  343.3 76.4 reduce-scatter.31
  469.5 74.6 reduce-scatter.29
  547.6 76.4 reduce-scatter.25
  627.5 76.4 reduce-scatter.23
  708.0 42.4 reduce-scatter.21
  754.6 42.4 reduce-scatter.19
  800.5 65.4 reduce-scatter.17
  869.8 65.4 reduce-scatter.15
  937.5 55.8 all-reduce.35
  995.6 28.7 reduce-scatter.27
  1027.2 19.8 reduce-scatter.35
  1050.0 31.7 reduce-scatter.33
  1084.1 40.3 all-gather.36
  1126.1 30.6 all-gather.34
where the time goes:
time: 1180 us; the launch traced here: 1170 us
  waiting for transfers between devices  514 us (44%)
  matrix products  238 us (20%)
  blocking collectives  172 us (15%)
  local copies, waits for them, and re-layouts  122 us (10%)
  other arithmetic  57.3 us (5%)
  starting transfers between devices  41.5 us (4%)
  between operations  21.4 us (2%)
    reduce_scatter x2, waiting for transfers between devices, fsdp_layer_sum(): lax.psum_scatter(grad_w_qkv, 'fsdp', scatter_dimension=0, tiled=True)  134 us
    reduce_scatter x2, waiting for transfers between devices, fsdp_layer_sum(): lax.psum_scatter(grad_w_out, 'fsdp', scatter_dimension=0, tiled=True)  89.3 us
    reduce_scatter x2, waiting for transfers between devices, fsdp_layer_sum(): lax.psum_scatter(grad_w_up, 'fsdp', scatter_dimension=0, tiled=True)  81.7 us
    unnamed x337, local copies, waits for them, and re-layouts  63.4 us
    unnamed x25, waiting for transfers between devices  54.6 us
    unnamed x2, blocking collectives  52.7 us
    all_gather x2, waiting for transfers between devices, gather_layer(): lax.all_gather(w_down, 'fsdp', axis=0, tiled=True)  39.8 us
    all_gather x1, blocking collectives, seq_total_sum(): lax.all_gather(pieces[0].astype(jnp.bfloat16), 'seq', axis=2, tiled=True)  35.1 us
  transfers between devices with their start and end apart: 31, of which 19 were waited for; matrix products, arithmetic and copies ran while one was open for 32% of the time, Pallas kernels for 0%

commit v1 on v0

--- a/solution.py
+++ b/solution.py
@@ -310,18 +310,18 @@
         grad_shift_ffn,
     ) = weight_grads
     return (
-        lax.psum_scatter(grad_w_qkv, "fsdp", scatter_dimension=0, tiled=True),
-        lax.psum_scatter(grad_b_qv, "fsdp", scatter_dimension=0, tiled=True),
-        lax.psum_scatter(grad_w_out, "fsdp", scatter_dimension=0, tiled=True),
-        lax.psum_scatter(grad_b_out, "fsdp", scatter_dimension=0, tiled=True),
-        lax.psum_scatter(grad_gain_attn, "fsdp", scatter_dimension=0, tiled=True),
-        lax.psum_scatter(grad_shift_attn, "fsdp", scatter_dimension=0, tiled=True),
-        lax.psum_scatter(grad_w_up, "fsdp", scatter_dimension=0, tiled=True),
-        lax.psum_scatter(grad_b_up, "fsdp", scatter_dimension=0, tiled=True),
-        lax.psum_scatter(grad_w_down, "fsdp", scatter_dimension=0, tiled=True),
-        lax.psum_scatter(grad_b_down, "fsdp", scatter_dimension=0, tiled=True),
-        lax.psum_scatter(grad_gain_ffn, "fsdp", scatter_dimension=0, tiled=True),
-        lax.psum_scatter(grad_shift_ffn, "fsdp", scatter_dimension=0, tiled=True),
+        lax.psum_scatter(grad_w_qkv.astype(jnp.bfloat16), "fsdp", scatter_dimension=0, tiled=True),
+        lax.psum_scatter(grad_b_qv.astype(jnp.bfloat16), "fsdp", scatter_dimension=0, tiled=True),
+        lax.psum_scatter(grad_w_out.astype(jnp.bfloat16), "fsdp", scatter_dimension=0, tiled=True),
+        lax.psum_scatter(grad_b_out.astype(jnp.bfloat16), "fsdp", scatter_dimension=0, tiled=True),
+        lax.psum_scatter(grad_gain_attn.astype(jnp.bfloat16), "fsdp", scatter_dimension=0, tiled=True),
+        lax.psum_scatter(grad_shift_attn.astype(jnp.bfloat16), "fsdp", scatter_dimension=0, tiled=True),
+        lax.psum_scatter(grad_w_up.astype(jnp.bfloat16), "fsdp", scatter_dimension=0, tiled=True),
+        lax.psum_scatter(grad_b_up.astype(jnp.bfloat16), "fsdp", scatter_dimension=0, tiled=True),
+        lax.psum_scatter(grad_w_down.astype(jnp.bfloat16), "fsdp", scatter_dimension=0, tiled=True),
+        lax.psum_scatter(grad_b_down.astype(jnp.bfloat16), "fsdp", scatter_dimension=0, tiled=True),
+        lax.psum_scatter(grad_gain_ffn.astype(jnp.bfloat16), "fsdp", scatter_dimension=0, tiled=True),
+        lax.psum_scatter(grad_shift_ffn.astype(jnp.bfloat16), "fsdp", scatter_dimension=0, tiled=True),
     )
 
 
@@ -442,17 +442,16 @@
         gain_ffn,
         shift_ffn,
     )
-    layer_inputs = []
+    kept = []
     for layer_index in range(LAYERS):
         weights = gather_layer(stacks, layer_index)
-        layer_inputs.append(hidden)
         hidden, stored = layer_forward(hidden, weights, key_live)
+        kept.append((weights, stored))
     result = jnp.where(row_live, hidden, 0.0)
     grad_hidden = jnp.where(row_live, cotangent, 0.0)
     collected = []
     for layer_index in reversed(range(LAYERS)):
-        weights = gather_layer(stacks, layer_index)
-        stored = layer_forward(layer_inputs[layer_index], weights, key_live)[1]
+        weights, stored = kept[layer_index]
         grad_hidden, weight_grads = layer_backward(grad_hidden, weights, stored, key_live)
         collected.insert(0, fsdp_layer_sum(weight_grads))
     stacked_grads = tuple((jnp.stack(member) for member in zip(*collected)))

time: 1180 us -> 1050 us (0.89)
  matrix products: 238 us -> 157 us
  local copies, waits for them, and re-layouts: 122 us -> 107 us
  waiting for transfers between devices: 514 us -> 502 us
    reduce_scatter x8, waiting for transfers between devices: 306 us -> 231 us  [the longest x2 110 us: fsdp_layer_sum(): lax.psum_scatter(grad_w_up.astype(jnp.bfloat16), 'fsdp', scatter_dimensio...]
    all_to_all x2, waiting for transfers between devices: 25.7 us -> 54.7 us  [layer_forward(): lax.all_to_all(projected.reshape(local_rows, 3, groups, local_heads, HD),...]
    dot_general x4 -> x2, matrix products: 32.5 us -> 8.78 us  [layer_forward(): jnp.dot(active, w_down, preferred_element_type=jnp.float32)]
    sub x4 -> x0, matrix products: 18.6 us -> none  [one_block(): exponent = jnp.exp(scores - top_score)]
    dot_general x8 -> x4, matrix products: 23.7 us -> 7.87 us  [one_block(): jnp.einsum('hqk,khd->qhd', probability, values_all, preferred_element_typ...]
    all_to_all x1, waiting for transfers between devices: 10 us -> 25.5 us  [layer_backward(): lax.all_to_all(grad_stack, 'seq', split_axis=0, concat_axis=2, tiled=True)]
    unnamed x337 -> x331, local copies, waits for them, and re-layouts: 63.4 us -> 53.7 us
  transfers between devices with their start and end apart: 31 -> 29, of which waited for: 19 -> 18; matrix products, arithmetic and copies ran while one was open for 32% -> 23% of each run, Pallas kernels for 0% -> 0%
where the time goes in v1:
time: 1050 us; the launch traced here: 1040 us
  waiting for transfers between devices  502 us (48%)
  blocking collectives  172 us (16%)
  matrix products  157 us (15%)
  local copies, waits for them, and re-layouts  107 us (10%)
  other arithmetic  46.6 us (4%)
  starting transfers between devices  30.3 us (3%)
  between operations  21.5 us (2%)
    reduce_scatter x2, waiting for transfers between devices, fsdp_layer_sum(): lax.psum_scatter(grad_w_up.astype(jnp.bfloat16), 'fsdp', scatter_dimensio...  110 us
    reduce_scatter x2, waiting for transfers between devices, fsdp_layer_sum(): lax.psum_scatter(grad_w_qkv.astype(jnp.bfloat16), 'fsdp', scatter_dimensi...  100 us
    unnamed x25, waiting for transfers between devices  64.5 us
    all_to_all x2, waiting for transfers between devices, layer_forward(): lax.all_to_all(projected.reshape(local_rows, 3, groups, local_heads, HD),...  54.7 us
    unnamed x331, local copies, waits for them, and re-layouts  53.7 us
    unnamed x2, blocking collectives  51.8 us
    all_gather x2, waiting for transfers between devices, gather_layer(): lax.all_gather(w_down, 'fsdp', axis=0, tiled=True)  49.4 us
    all_gather x1, blocking collectives, seq_total_sum(): lax.all_gather(pieces[0].astype(jnp.bfloat16), 'seq', axis=2, tiled=True)  35.6 us
  transfers between devices with their start and end apart: 29, of which 18 were waited for; matrix products, arithmetic and copies ran while one was open for 23% of the time, Pallas kernels for 0%

profile of v1, /device:TPU:0, one launch (start us, length us, event | category | flops | bytes accessed | tf_op | source)
XLA Modules:
  0.0 1036.0 jit_solution(11128718490062350415)
XLA Ops:
  20.4 26.5 %all-reduce.32 = (bf16[1536]{0:T(1024)(128)(2,1)S(1)}, bf16[768]{0:T(1024)(128)(2,1)}, bf16[768]{0:T(1024)(128)(2,1)}, bf16[768]{0:T(1024)(128)(2,1)S(1)}, bf16[...) all-reduce(bf16[1536]{0:T(1024)(128)(2,1)S(1)} %dynamic-update-slic, ...), channel_id=3, replica_groups=mesh['fsdp'=8,'seq'=4] {'fsdp'}, use_global_device_ids=true, to_apply=%add | all-reduce | flops 11520 | bytes 46080
  53.8 4.8 all-to-all-start
  59.4 26.5 %all-to-all-done = bf16[256,3,4,3,64]{0,4,3,1,2:T(8,128)(2,1)S(1)} async-done(((bf16[256,3,4,3,64]{0,4,3,1,2:T(8,128)(2,1)}), bf16[256,3,4,3,64]{0,4,3,1,2:T(8,128)(2,1)S(1)}, u32[]{:S(2)}, u32[]{:S(2)}) %all-to-all-start) | async-done | bytes 1179680 | tf_op jit(solution)/shard_map/all_to_all | solution.py:160
  86.5 9.5 while.56
  104.3 9.1 all-gather.7
  118.5 11.6 %multiply_convert_fusion.3 = (bf16[256,3072]{1,0:T(8,128)(2,1)}, f32[256,3072]{1,0:T(8,128)}, f32[256,3072]{1,0:T(8,128)}) fusion(f32[3072]{0:T(1024)S(1)} %bitcast.463, bf16[1,768,3072]{2,1,0:T(8,128)(2,1)} %all-gather.43.cloned.1.call-done, f32[256,768]{1,0:T(8,128)S(1)} %get-tuple-element.765, f32[768]{0:T(1024)S(1)} %convert_element_type.363, ...), kind=kOutput, calls=%fused_computation.155 | convolution fusion | flops 1260847104 | bytes 13389824 | tf_op jit(solution)/shard_map/dot_general | solution.py:182
  130.1 26.2 %all-gather.45.cloned.1.call-done = bf16[1,3072,768]{2,1,0:T(8,128)(2,1)} async-done(((bf16[1,384,768]{2,1,0:T(8,128)(2,1)}), bf16[1,3072,768]{2,1,0:T(8,128)(2,1)}) %all-gather.45.cloned.1.call-update) | async-done | bytes 4718608 | tf_op jit(solution)/shard_map/all_gather | solution.py:54
  156.3 4.3 fusion.213
  160.9 31.7 %all-gather.47.cloned.1.call-done = bf16[1,768,2304]{2,1,0:T(8,128)(2,1)} async-done(((bf16[1,96,2304]{2,1,0:T(8,128)(2,1)}), bf16[1,768,2304]{2,1,0:T(8,128)(2,1)}) %all-gather.47.cloned.1.call-update) | async-done | bytes 3538960 | tf_op jit(solution)/shard_map/all_gather | solution.py:46
  197.5 4.6 all-to-all-start.2
  202.8 28.2 %all-to-all-done.2 = bf16[256,3,4,3,64]{0,4,3,1,2:T(8,128)(2,1)S(1)} async-done(((bf16[256,3,4,3,64]{0,4,3,1,2:T(8,128)(2,1)}), bf16[256,3,4,3,64]{0,4,3,1,2:T(8,128)(2,1)S(1)}, u32[]{:S(2)}, u32[]{:S(2)}) %all-to-all-start.2) | async-done | bytes 1179680 | tf_op jit(solution)/shard_map/all_to_all | solution.py:160
  231.7 9.5 while.57
  249.4 8.7 all-gather.19
  266.1 12.0 %multiply_convert_fusion.2 = (bf16[256,3072]{1,0:T(8,128)(2,1)}, f32[256,3072]{1,0:T(8,128)}, f32[256,3072]{1,0:T(8,128)}) fusion(f32[3072]{0:T(1024)} %bitcast.462, bf16[1,768,3072]{2,1,0:T(8,128)(2,1)} %all-gather.51.cloned.1.call-done, f32[256,768]{1,0:T(8,128)S(1)} %get-tuple-element.770, f32[768]{0:T(1024)S(1)} %convert_element_type.370, ...), kind=kOutput, calls=%fused_computation.142 | convolution fusion | flops 1260847104 | bytes 13389824 | tf_op jit(solution)/shard_map/dot_general | solution.py:182
  278.2 23.1 %all-gather.53.cloned.1.call-done = bf16[1,3072,768]{2,1,0:T(8,128)(2,1)} async-done(((bf16[1,384,768]{2,1,0:T(8,128)(2,1)}), bf16[1,3072,768]{2,1,0:T(8,128)(2,1)}) %all-gather.53.cloned.1.call-update) | async-done | bytes 4718608 | tf_op jit(solution)/shard_map/all_gather | solution.py:54
  301.4 4.5 fusion.215
  316.1 4.8 all-to-all-start.4
  320.9 12.1 %all-to-all-done.4 = bf16[256,4,3,64]{0,3,2,1:T(8,128)(2,1)S(1)} async-done(((bf16[256,4,3,64]{0,3,2,1:T(8,128)(2,1)}), bf16[256,4,3,64]{0,3,2,1:T(8,128)(2,1)S(1)}, u32[]{:S(2)}, u32[]{:S(2)}) %all-to-all-start.4) | async-done | bytes 393248 | tf_op jit(solution)/shard_map/all_to_all | solution.py:254
  334.4 27.6 %while.58 = (s32[]{:T(128)}, f32[1024,3,64]{0,2,1:T(8,128)}, f32[1024,3,64]{0,2,1:T(8,128)}, bf16[2,512,3,64]{1,3,2,0:T(8,128)(2,1)}, bf16[2,512,3,64]{1,3,2,0:T...) while((s32[]{:T(128)}, f32[1024,3,64]{0,2,1:T(8,128)}, ...), condition=%wide.region_22.23_spmd.clone, body=%wide.region_20.22_spmd.clone.sunk | while | flops 1031306752 | bytes 112519104 | solution.py:132
  366.2 4.6 copy.169
  373.9 4.3 all-to-all-start.5
  380.8 25.5 %all-to-all-done.5 = bf16[4,2,73728]{2,1,0:T(2,128)(2,1)} async-done(((bf16[4,2,73728]{2,1,0:T(2,128)(2,1)}), bf16[4,2,73728]{2,1,0:T(2,128)(2,1)}, u32[]{:S(2)}, u32[]{:S(2)}) %all-to-all-start.5) | async-done | bytes 1179680 | tf_op jit(solution)/shard_map/all_to_all | solution.py:267
  406.3 3.9 reshape.563
  410.2 3.8 copy.195
  415.7 4.6 multiply_reduce_fusion.3
  422.3 5.2 fusion.217
  433.5 5.1 convolution_convert_fusion
  439.6 5.1 convolution_convert_fusion.1
  445.9 5.1 convolution_convert_fusion.2
  451.7 5.3 convolution_convert_fusion.3
  467.6 7.6 all-to-all-done.6
  476.6 29.7 %while.59 = (s32[]{:T(128)}, f32[1024,3,64]{0,2,1:T(8,128)}, f32[1024,3,64]{0,2,1:T(8,128)}, bf16[2,512,3,64]{1,3,2,0:T(8,128)(2,1)}, bf16[2,512,3,64]{1,3,2,0:T...) while((s32[]{:T(128)}, f32[1024,3,64]{0,2,1:T(8,128)}, ...), condition=%wide.region_29.30_spmd.clone, body=%wide.region_27.29_spmd.clone.sunk | while | flops 1031306752 | bytes 107792680 | solution.py:132
  510.5 4.6 copy.177
  518.2 30.9 %all_to_all.126 = bf16[4,2,73728]{2,1,0:T(2,128)(2,1)} all-to-all(bf16[4,2,73728]{2,1,0:T(2,128)(2,1)} %reshape.564), channel_id=1, replica_groups=mesh['fsdp'=8,'seq'=4] {'seq'}, dimensions={0} | all-to-all | bytes 2359296 | tf_op jit(solution)/shard_map/all_to_all | solution.py:267
  563.4 20.1 %reduce-scatter.30.cloned.1.call-done = bf16[384,768]{1,0:T(8,128)(2,1)} async-done(((bf16[3072,768]{1,0:T(8,128)(2,1)}), bf16[384,768]{1,0:T(8,128)(2,1)}) %reduce-scatter.30.cloned.1.call-update) | async-done | bytes 589840 | tf_op jit(solution)/shard_map/reduce_scatter | solution.py:321
  588.1 52.9 %reduce-scatter.26.cloned.1.call-done = bf16[96,3072]{1,0:T(8,128)(2,1)} async-done(((bf16[768,3072]{1,0:T(8,128)(2,1)}), bf16[96,3072]{1,0:T(8,128)(2,1)}) %reduce-scatter.26.cloned.1.call-update) | async-done | bytes 589840 | tf_op jit(solution)/shard_map/reduce_scatter | solution.py:319
  640.9 57.6 %reduce-scatter.24.cloned.1.call-done = bf16[96,3072]{1,0:T(8,128)(2,1)} async-done(((bf16[768,3072]{1,0:T(8,128)(2,1)}), bf16[96,3072]{1,0:T(8,128)(2,1)}) %reduce-scatter.24.cloned.1.call-update) | async-done | bytes 589840 | tf_op jit(solution)/shard_map/reduce_scatter | solution.py:319
  701.0 49.0 %reduce-scatter.18.cloned.1.call-done = bf16[96,2304]{1,0:T(8,128)(2,1)} async-done(((bf16[768,2304]{1,0:T(8,128)(2,1)}), bf16[96,2304]{1,0:T(8,128)(2,1)}) %reduce-scatter.18.cloned.1.call-update) | async-done | bytes 442384 | tf_op jit(solution)/shard_map/reduce_scatter | solution.py:313
  750.0 51.4 %reduce-scatter.16.cloned.1.call-done = bf16[96,2304]{1,0:T(8,128)(2,1)} async-done(((bf16[768,2304]{1,0:T(8,128)(2,1)}), bf16[96,2304]{1,0:T(8,128)(2,1)}) %reduce-scatter.16.cloned.1.call-update) | async-done | bytes 442384 | tf_op jit(solution)/shard_map/reduce_scatter | solution.py:313
  818.4 6.4 reduce-scatter.36.cloned.1.call-done
  825.8 55.5 %all-reduce.36.cloned.1.call-done = bf16[2,384,768]{1,0,2:T(2,128)(2,1)} async-done(((bf16[2,384,768]{1,0,2:T(2,128)(2,1)}), bf16[2,384,768]{1,0,2:T(2,128)(2,1)}) %all-reduce.36.cloned.1.call-update) | async-done | bytes 1179664
  883.4 25.3 %all-reduce.31 = (bf16[768]{0:T(1024)(128)(2,1)S(1)}, bf16[1536]{0:T(1024)(128)(2,1)S(1)}, bf16[1536]{0:T(1024)(128)(2,1)S(1)}, bf16[768]{0:T(1024)(128)(2,1)S(1...) all-reduce(bf16[768]{0:T(1024)(128)(2,1)S(1)} %dynamic-update-slice, ...), channel_id=25, replica_groups=mesh['fsdp'=8,'seq'=4] {'fsdp'}, use_global_device_ids=true, to_apply=%add.13 | all-reduce | flops 19200 | bytes 76800
  912.5 17.2 %all_gather.109 = bf16[2,96,768]{1,0,2:T(2,128)(2,1)S(1)} all-gather(bf16[2,96,192]{1,0,2:T(2,128)(2,1)S(1)} %bitcast.459), channel_id=1, replica_groups=mesh['fsdp'=8,'seq'=4] {'seq'}, dimensions={2}, use_global_device_ids=true | all-gather | bytes 368640 | tf_op jit(solution)/shard_map/all_gather | solution.py:361
  931.3 4.1 broadcast_select_fusion
  935.9 18.2 %all-reduce.33 = (bf16[1,20,768]{2,1,0:T(8,128)(2,1)S(1)}, bf16[2,192]{1,0:T(2,128)(2,1)S(1)}, bf16[2,96]{1,0:T(2,128)(2,1)S(1)}, bf16[2,96]{1,0:T(2,128)(2,1)S(...) all-reduce(bf16[1,20,768]{2,1,0:T(8,128)(2,1)S(1)} %fusion.168, ...), channel_id=1, replica_groups=mesh['fsdp'=8,'seq'=4] {'seq'}, use_global_device_ids=true, to_apply=%region_30.31 | all-reduce | flops 17664 | bytes 70656 | tf_op jit(solution)/shard_map/psum | solution.py:380
  961.6 35.6 %all_gather.108 = bf16[2,96,2304]{1,0,2:T(2,128)(2,1)S(1)} all-gather(bf16[2,96,576]{1,0,2:T(2,128)(2,1)S(1)} %bitcast.452), channel_id=1, replica_groups=mesh['fsdp'=8,'seq'=4] {'seq'}, dimensions={2}, use_global_device_ids=true | all-gather | bytes 1105920 | tf_op jit(solution)/shard_map/all_gather | solution.py:358
  999.8 5.1 copy.190
  1004.9 21.0 %all-gather.35.cloned.1.call-done = bf16[2,96,3072]{2,1,0:T(8,128)(2,1)} async-done(((bf16[2,96,768]{2,1,0:T(8,128)(2,1)}), bf16[2,96,3072]{2,1,0:T(8,128)(2,1)}) %all-gather.35.cloned.1.call-update) | async-done | bytes 1179664 | tf_op jit(solution)/shard_map/all_gather | solution.py:364
  (675 shorter events, 240.0 us)
Async XLA Ops:
  7.2 41.5 %all-gather.39.cloned.1.call-start = ((), (), s32[]{:S(2)}) async-start(), calls=%async_computation.30 | async-start | bytes 3981312 | tf_op jit(solution)/shard_map/all_gather | solution.py:46
  9.6 106.6 %all-gather.41.cloned.1.call-start = ((), (), s32[]{:S(2)}) async-start(), calls=%async_computation.31 | async-start | bytes 1327104 | tf_op jit(solution)/shard_map/all_gather | solution.py:48
  11.5 107.0 %all-gather.43.cloned.1.call-start = ((), (), s32[]{:S(2)}) async-start(), calls=%async_computation.32 | async-start | bytes 5308416 | tf_op jit(solution)/shard_map/all_gather | solution.py:52
  12.6 143.7 %all-gather.45.cloned.1.call-start = ((), (), s32[]{:S(2)}) async-start(), calls=%async_computation.33 | async-start | bytes 5308416 | tf_op jit(solution)/shard_map/all_gather | solution.py:54
  13.8 178.8 %all-gather.47.cloned.1.call-start = ((), (), s32[]{:S(2)}) async-start(), calls=%async_computation.34 | async-start | bytes 3981312 | tf_op jit(solution)/shard_map/all_gather | solution.py:46
  14.4 249.4 %all-gather.49.cloned.1.call-start = ((), (), s32[]{:S(2)}) async-start(), calls=%async_computation.35 | async-start | bytes 1327104 | tf_op jit(solution)/shard_map/all_gather | solution.py:48
  53.8 32.0 %all-to-all-start = ((bf16[256,3,4,3,64]{0,4,3,1,2:T(8,128)(2,1)}), bf16[256,3,4,3,64]{0,4,3,1,2:T(8,128)(2,1)S(1)}, u32[]{:S(2)}, u32[]{:S(2)}) async-start(bf16[256,3,4,3,64]{0,4,3,1,2:T(8,128)(2,1)} %copy.149), calls=%async_computation | async-start | bytes 2359296 | tf_op jit(solution)/shard_map/all_to_all | solution.py:160
  58.6 207.5 %all-gather.51.cloned.1.call-start = ((), (), s32[]{:S(2)}) async-start(), calls=%async_computation.36 | async-start | bytes 5308416 | tf_op jit(solution)/shard_map/all_gather | solution.py:52
  100.1 14.6 %all-to-all-start.1 = ((bf16[4,2,24576]{2,1,0:T(2,128)(2,1)}), bf16[4,2,24576]{2,1,0:T(2,128)(2,1)S(1)}, u32[]{:S(2)}, u32[]{:S(2)}) async-start(bf16[4,2,24576]{2,1,0:T(2,128)(2,1)} %reshape.558), calls=%async_computation.1 | async-start | bytes 786432 | tf_op jit(solution)/shard_map/all_to_all | solution.py:170
  113.4 150.4 %copy-start.58 = (f32[768]{0:T(1024)}, f32[768]{0:T(1024)S(1)}, u32[]{:S(2)}) copy-start(f32[768]{0:T(1024)S(1)} %convert_element_type.366) | copy-start | bytes 9220
  160.6 103.2 %copy-start.25 = (f32[256,768]{1,0:T(8,128)}, f32[256,768]{1,0:T(8,128)S(1)}, u32[]{:S(2)}) copy-start(f32[256,768]{1,0:T(8,128)S(1)} %get-tuple-element.768) | copy-start | bytes 2359300
  197.5 33.6 %all-to-all-start.2 = ((bf16[256,3,4,3,64]{0,4,3,1,2:T(8,128)(2,1)}), bf16[256,3,4,3,64]{0,4,3,1,2:T(8,128)(2,1)S(1)}, u32[]{:S(2)}, u32[]{:S(2)}) async-start(bf16[256,3,4,3,64]{0,4,3,1,2:T(8,128)(2,1)} %copy.157), calls=%async_computation.2 | async-start | bytes 2359296 | tf_op jit(solution)/shard_map/all_to_all | solution.py:160
  202.1 99.2 %all-gather.53.cloned.1.call-start = ((), (), s32[]{:S(2)}) async-start(), calls=%async_computation.37 | async-start | bytes 5308416 | tf_op jit(solution)/shard_map/all_gather | solution.py:54
  245.3 15.2 %all-to-all-start.3 = ((bf16[4,2,24576]{2,1,0:T(2,128)(2,1)}), bf16[4,2,24576]{2,1,0:T(2,128)(2,1)S(1)}, u32[]{:S(2)}, u32[]{:S(2)}) async-start(bf16[4,2,24576]{2,1,0:T(2,128)(2,1)} %reshape.560), calls=%async_computation.3 | async-start | bytes 786432 | tf_op jit(solution)/shard_map/all_to_all | solution.py:170
  316.1 16.9 %all-to-all-start.4 = ((bf16[256,4,3,64]{0,3,2,1:T(8,128)(2,1)}), bf16[256,4,3,64]{0,3,2,1:T(8,128)(2,1)S(1)}, u32[]{:S(2)}, u32[]{:S(2)}) async-start(bf16[256,4,3,64]{0,3,2,1:T(8,128)(2,1)} %bitcast.44), calls=%async_computation.4 | async-start | bytes 786432 | tf_op jit(solution)/shard_map/all_to_all | solution.py:254
  373.9 32.4 %all-to-all-start.5 = ((bf16[4,2,73728]{2,1,0:T(2,128)(2,1)}), bf16[4,2,73728]{2,1,0:T(2,128)(2,1)}, u32[]{:S(2)}, u32[]{:S(2)}) async-start(bf16[4,2,73728]{2,1,0:T(2,128)(2,1)} %reshape.562), calls=%async_computation.5 | async-start | bytes 2359296 | tf_op jit(solution)/shard_map/all_to_all | solution.py:267
  378.2 182.7 %reduce-scatter.22.cloned.1.call-start = ((), (), s32[]{:S(2)}) async-start(), calls=%async_computation.22 | async-start | bytes 1327104 | tf_op jit(solution)/shard_map/reduce_scatter | solution.py:315
  380.8 180.2 %reduce-scatter.20.cloned.1.call-start = ((), (), s32[]{:S(2)}) async-start(), calls=%async_computation.21 | async-start | bytes 1327104 | tf_op jit(solution)/shard_map/reduce_scatter | solution.py:315
  433.4 130.0 %reduce-scatter.32.cloned.1.call-start = ((), (), s32[]{:S(2)}) async-start(), calls=%async_computation.28 | async-start | bytes 5308416 | tf_op jit(solution)/shard_map/reduce_scatter | solution.py:321
  438.6 144.9 %reduce-scatter.30.cloned.1.call-start = ((), (), s32[]{:S(2)}) async-start(), calls=%async_computation.27 | async-start | bytes 5308416 | tf_op jit(solution)/shard_map/reduce_scatter | solution.py:321
  444.8 196.1 %reduce-scatter.26.cloned.1.call-start = ((), (), s32[]{:S(2)}) async-start(), calls=%async_computation.24 | async-start | bytes 5308416 | tf_op jit(solution)/shard_map/reduce_scatter | solution.py:319
  451.0 247.5 %reduce-scatter.24.cloned.1.call-start = ((), (), s32[]{:S(2)}) async-start(), calls=%async_computation.23 | async-start | bytes 5308416 | tf_op jit(solution)/shard_map/reduce_scatter | solution.py:319
  460.7 14.5 %all-to-all-start.6 = ((bf16[256,4,3,64]{0,3,2,1:T(8,128)(2,1)}), bf16[256,4,3,64]{0,3,2,1:T(8,128)(2,1)S(1)}, u32[]{:S(2)}, u32[]{:S(2)}) async-start(bf16[256,4,3,64]{0,3,2,1:T(8,128)(2,1)} %bitcast.52), calls=%async_computation.6 | async-start | bytes 786432 | tf_op jit(solution)/shard_map/all_to_all | solution.py:254
  464.2 285.8 %reduce-scatter.18.cloned.1.call-start = ((), (), s32[]{:S(2)}) async-start(), calls=%async_computation.20 | async-start | bytes 3981312 | tf_op jit(solution)/shard_map/reduce_scatter | solution.py:313
  467.4 334.0 %reduce-scatter.16.cloned.1.call-start = ((), (), s32[]{:S(2)}) async-start(), calls=%async_computation.19 | async-start | bytes 3981312 | tf_op jit(solution)/shard_map/reduce_scatter | solution.py:313
  560.8 263.9 %reduce-scatter.36.cloned.1.call-start = ((), (), s32[]{:S(2)}) async-start(), calls=%async_computation.39 | async-start | bytes 491520
  563.4 317.9 %all-reduce.36.cloned.1.call-start = ((), (), s32[]{:S(2)}) async-start(), calls=%async_computation.40 | async-start | bytes 2359296
  587.8 324.7 %reduce-scatter.28.cloned.1.call-start = ((), (), s32[]{:S(2)}) async-start(), calls=%async_computation.25 | async-start | bytes 1474560 | tf_op jit(solution)/shard_map/reduce_scatter | solution.py:350
  701.0 259.5 %reduce-scatter.34.cloned.1.call-start = ((), (), s32[]{:S(2)}) async-start(), calls=%async_computation.38 | async-start | bytes 1474560
  811.0 72.2 %copy-start.99 = (bf16[768]{0:T(1024)(128)(2,1)S(1)}, bf16[768]{0:T(1024)(128)(2,1)}, u32[]{:S(2)}) copy-start(bf16[768]{0:T(1024)(128)(2,1)} %get-tuple-element.575) | copy-start | bytes 4612
  811.0 72.2 %copy-start.100 = (bf16[768]{0:T(1024)(128)(2,1)S(1)}, bf16[768]{0:T(1024)(128)(2,1)}, u32[]{:S(2)}) copy-start(bf16[768]{0:T(1024)(128)(2,1)} %get-tuple-element.583) | copy-start | bytes 4612
  811.0 72.2 %copy-start.101 = (bf16[768]{0:T(1024)(128)(2,1)S(1)}, bf16[768]{0:T(1024)(128)(2,1)}, u32[]{:S(2)}) copy-start(bf16[768]{0:T(1024)(128)(2,1)} %get-tuple-element.702) | copy-start | bytes 4612
  811.0 72.3 %copy-start.102 = (bf16[768]{0:T(1024)(128)(2,1)S(1)}, bf16[768]{0:T(1024)(128)(2,1)}, u32[]{:S(2)}) copy-start(bf16[768]{0:T(1024)(128)(2,1)} %get-tuple-element.706) | copy-start | bytes 4612
  811.0 72.3 %copy-start.103 = (bf16[768]{0:T(1024)(128)(2,1)S(1)}, bf16[768]{0:T(1024)(128)(2,1)}, u32[]{:S(2)}) copy-start(bf16[768]{0:T(1024)(128)(2,1)} %get-tuple-element.700) | copy-start | bytes 4612
  811.1 72.3 %copy-start.104 = (bf16[768]{0:T(1024)(128)(2,1)S(1)}, bf16[768]{0:T(1024)(128)(2,1)}, u32[]{:S(2)}) copy-start(bf16[768]{0:T(1024)(128)(2,1)} %get-tuple-element.704) | copy-start | bytes 4612
  811.1 72.3 %copy-start.107 = (bf16[3072]{0:T(1024)(128)(2,1)S(1)}, bf16[3072]{0:T(1024)(128)(2,1)}, u32[]{:S(2)}) copy-start(bf16[3072]{0:T(1024)(128)(2,1)} %get-tuple-element.777) | copy-start | bytes 18436
  811.1 72.3 %copy-start.108 = (bf16[3072]{0:T(1024)(128)(2,1)S(1)}, bf16[3072]{0:T(1024)(128)(2,1)}, u32[]{:S(2)}) copy-start(bf16[3072]{0:T(1024)(128)(2,1)} %get-tuple-element.779) | copy-start | bytes 18436
  811.1 72.3 %copy-start.115 = (bf16[768]{0:T(1024)(128)(2,1)S(1)}, bf16[768]{0:T(1024)(128)(2,1)}, u32[]{:S(2)}) copy-start(bf16[768]{0:T(1024)(128)(2,1)} %get-tuple-element.581) | copy-start | bytes 4612
  811.1 72.3 %copy-start.116 = (bf16[768]{0:T(1024)(128)(2,1)S(1)}, bf16[768]{0:T(1024)(128)(2,1)}, u32[]{:S(2)}) copy-start(bf16[768]{0:T(1024)(128)(2,1)} %get-tuple-element.586) | copy-start | bytes 4612
  811.1 72.3 %copy-start.117 = (bf16[768]{0:T(1024)(128)(2,1)S(1)}, bf16[768]{0:T(1024)(128)(2,1)}, u32[]{:S(2)}) copy-start(bf16[768]{0:T(1024)(128)(2,1)} %get-tuple-element.577) | copy-start | bytes 4612
  811.1 72.3 %copy-start.118 = (bf16[768]{0:T(1024)(128)(2,1)S(1)}, bf16[768]{0:T(1024)(128)(2,1)}, u32[]{:S(2)}) copy-start(bf16[768]{0:T(1024)(128)(2,1)} %get-tuple-element.584) | copy-start | bytes 4612
  811.1 72.3 %copy-start.119 = (bf16[768]{0:T(1024)(128)(2,1)S(1)}, bf16[768]{0:T(1024)(128)(2,1)}, u32[]{:S(2)}) copy-start(bf16[768]{0:T(1024)(128)(2,1)} %get-tuple-element.579) | copy-start | bytes 4612
  811.1 72.3 %copy-start.120 = (bf16[768]{0:T(1024)(128)(2,1)S(1)}, bf16[768]{0:T(1024)(128)(2,1)}, u32[]{:S(2)}) copy-start(bf16[768]{0:T(1024)(128)(2,1)} %get-tuple-element.585) | copy-start | bytes 4612
  811.2 188.6 %all-gather.37.cloned.1.call-start = ((), (), s32[]{:S(2)}) async-start(), calls=%async_computation.29 | async-start | bytes 1474560 | tf_op jit(solution)/shard_map/all_gather | solution.py:367
  814.7 116.5 %copy-start.69 = (f32[256]{0:T(256)S(1)}, f32[256]{0:T(256)}, u32[]{:S(2)}) copy-start(f32[256]{0:T(256)} %copy-done.68) | copy-start | bytes 3076
  814.8 116.5 %copy-start.91 = (pred[256]{0:T(512)(128)(4,1)S(1)}, pred[256]{0:T(512)(128)(4,1)}, u32[]{:S(2)}) copy-start(pred[256]{0:T(512)(128)(4,1)} %copy-done.90) | copy-start | bytes 772
  815.5 115.7 %copy-start.30 = (f32[256,768]{1,0:T(8,128)S(1)}, f32[256,768]{1,0:T(8,128)}, u32[]{:S(2)}) copy-start(f32[256,768]{1,0:T(8,128)} %copy-done.29) | copy-start | bytes 2359300
  883.2 142.7 %all-gather.35.cloned.1.call-start = ((), (), s32[]{:S(2)}) async-start(), calls=%async_computation.26 | async-start | bytes 1474560 | tf_op jit(solution)/shard_map/all_gather | solution.py:364
  (145 other events, 1499.2 us)
Sparse Core Ops, SparseCore 0:
  10.5 36.9 all-gather.38
  49.3 24.0 all-gather.40
  75.9 39.0 all-gather.42
  117.4 38.9 all-gather.44
  158.6 33.9 all-gather.46
  194.3 24.0 all-gather.48
  220.9 38.9 all-gather.50
  262.4 38.9 all-gather.52
  382.2 37.2 reduce-scatter.21
  433.5 35.0 reduce-scatter.19
  472.1 53.8 reduce-scatter.31
  529.7 53.8 reduce-scatter.29
  587.0 53.8 reduce-scatter.25
  644.6 53.8 reduce-scatter.23
  701.8 48.0 reduce-scatter.17
  753.3 48.0 reduce-scatter.15
  804.1 20.5 reduce-scatter.35
  827.1 54.1 all-reduce.35
  883.7 28.7 reduce-scatter.27
  915.3 29.8 reduce-scatter.33
  947.5 45.8 all-gather.36
  995.0 30.8 all-gather.34

commit v2 on v1

--- a/solution.py
+++ b/solution.py
@@ -1,19 +1,365 @@
+import functools
 import math
 
 import jax
 import jax.numpy as jnp
 from jax import lax
+from jax.experimental import pallas as pl
+from jax.experimental.pallas import tpu as pltpu
 from jax.sharding import PartitionSpec as P
 
 D = 768
 HEADS = 12
 HD = 64
+FF = 3072
 MEM = 10
 LAYERS = 2
-
+GROUP = 640
+CTX = 256
+MESH = pl.DeviceIdType.MESH
 
 norm_eps = 1e-12
 masked_score = -1e30
+
+
+def dot(a, b):
+    return jnp.dot(a, b, preferred_element_type=jnp.float32)
+
+
+def dot_t(a, b):
+    return lax.dot_general(a, b, (((1,), (1,)), ((), ())), preferred_element_type=jnp.float32)
+
+
+def t_dot(a, b):
+    return lax.dot_general(a, b, (((0,), (0,)), ((), ())), preferred_element_type=jnp.float32)
+
+
+def standardize(values):
+    row_mean = jnp.mean(values, axis=-1, keepdims=True)
+    centred = values - row_mean
+    variance = jnp.mean(centred * centred, axis=-1, keepdims=True)
+    scale = lax.rsqrt(variance + norm_eps)
+    return centred * scale, scale
+
+
+B_OUT, GAIN_A, SHIFT_A, B_UP, B_DOWN, GAIN_F, SHIFT_F, VECS = 0, 1, 2, 3, 7, 8, 9, 10
+
+
+def forward_kernel(
+    n, g, *refs
+):
+    (
+        x0_ref, mask_ref, bqkv_ref, vec_ref, sq_ref, so_ref, su_ref, sd_ref,
+        y_ref, fq_ref, fo_ref, fu_ref, fd_ref, xb_out, heads_out, lse_out, ctx_out, r1_out, pre_out, act_out, r2_out,
+        wq, wo, wu, wd, x_s, xb, heads, lse, ctx, r1, pre, act, r2, acc_s, nb_s, qkv_send, ctx_send,
+        w_send, w_recv, c_send, c_recv, own_sem, q_send_sem, q_recv_sem, k_send_sem, k_recv_sem, save_sem,
+    ) = refs
+    f, s = lax.axis_index("fsdp"), lax.axis_index("seq")
+    rows = x0_ref.shape[0]
+    half = n // 2
+    partner = f + 1 - 2 * lax.rem(f, 2)
+
+    barrier = pltpu.get_barrier_semaphore()
+    for j in range(1, n):
+        pl.semaphore_signal(barrier, 1, device_id={"fsdp": lax.rem(f + j, n), "seq": s}, device_id_type=MESH)
+    for j in range(1, g):
+        pl.semaphore_signal(barrier, 1, device_id={"fsdp": f, "seq": lax.rem(s + j, g)}, device_id_type=MESH)
+    pl.semaphore_wait(barrier, n - 1 + g - 1)
+
+    lands = (wq, wo, wu, wd)
+    shards = (sq_ref, so_ref, su_ref, sd_ref)
+    fulls = (fq_ref, fo_ref, fu_ref, fd_ref)
+
+    def place(m, owner):
+        layer, kind = divmod(m, 4)
+        depth = shards[kind].shape[1]
+        return lands[kind].at[layer, pl.ds(pl.multiple_of(owner * depth, depth), depth)]
+
+    def to_chip(m, j):
+        layer, kind = divmod(m, 4)
+        return pltpu.make_async_remote_copy(
+            src_ref=shards[kind].at[layer], dst_ref=place(m, f), send_sem=w_send.at[m, j - 1], recv_sem=w_recv.at[m, j - 1],
+            device_id={"fsdp": lax.rem(f + 2 * j, n), "seq": s}, device_id_type=MESH)
+
+    def to_core(m, j):
+        owner = lax.rem(f - 2 * j + n, n)
+        return pltpu.make_async_remote_copy(
+            src_ref=place(m, owner), dst_ref=place(m, owner), send_sem=c_send.at[m, j], recv_sem=c_recv.at[m, j],
+            device_id={"fsdp": partner, "seq": s}, device_id_type=MESH)
+
+    def own_copy(m):
+        layer, kind = divmod(m, 4)
+        return pltpu.make_async_copy(shards[kind].at[layer], place(m, f), own_sem.at[m])
+
+    def save_full(m):
+        layer, kind = divmod(m, 4)
+        return pltpu.make_async_copy(lands[kind].at[layer], fulls[kind].at[layer], own_sem.at[m])
+
+    for m in range(4 * LAYERS):
+        own_copy(m).start()
+        for j in range(1, half):
+            to_chip(m, j).start()
+    for m in range(4 * LAYERS):
+        own_copy(m).wait()
+        to_core(m, 0).start()
+
+    def forward_on(m):
+        for j in range(1, half):
+            to_chip(m, j).wait_recv()
+            to_core(m, j).start()
+
+    def need(m):
+        for j in range(half):
+            to_core(m, j).wait_recv()
+        save_full(m).start()
+
+    saves = []
+
+    def save(src, dst):
+        copy = pltpu.make_async_copy(src, dst, save_sem.at[len(saves)])
+        copy.start()
+        saves.append(copy)
+
+    lane = lax.broadcasted_iota(jnp.int32, (rows, 128), 1)
+    x_s[...] = x0_ref[...]
+
+    for layer in range(LAYERS):
+        m0 = 4 * layer
+        xb[layer] = x_s[...].astype(jnp.bfloat16)
+        save(xb.at[layer], xb_out.at[layer])
+        forward_on(m0)
+        need(m0)
+
+        def q_copy(i):
+            return pltpu.make_async_remote_copy(
+                src_ref=qkv_send.at[i - 1], dst_ref=heads.at[layer, pl.ds(pl.multiple_of(s * rows, rows), rows)],
+                send_sem=q_send_sem.at[layer, i - 1], recv_sem=q_recv_sem.at[layer, i - 1],
+                device_id={"fsdp": f, "seq": lax.rem(s + i, g)}, device_id_type=MESH)
+
+        def q_arrival(i):
+            return pltpu.make_async_remote_copy(
+                src_ref=qkv_send.at[i - 1],
+                dst_ref=heads.at[layer, pl.ds(pl.multiple_of(lax.rem(s - i + g, g) * rows, rows), rows)],
+                send_sem=q_send_sem.at[layer, i - 1], recv_sem=q_recv_sem.at[layer, i - 1],
+                device_id={"fsdp": f, "seq": lax.rem(s + i, g)}, device_id_type=MESH)
+
+        if layer:
+            for i in range(1, g):
+                pltpu.make_async_remote_copy(
+                    src_ref=qkv_send.at[i - 1], dst_ref=heads.at[layer - 1, pl.ds(pl.multiple_of(s * rows, rows), rows)],
+                    send_sem=q_send_sem.at[layer - 1, i - 1], recv_sem=q_recv_sem.at[layer - 1, i - 1],
+                    device_id={"fsdp": f, "seq": lax.rem(s + i, g)}, device_id_type=MESH).wait_send()
+
+        for i in list(range(1, g)) + [0]:
+            group = lax.rem(s + i, g)
+            columns = pl.ds(pl.multiple_of(group * GROUP, 128), GROUP)
+            projected = (dot(xb[layer], wq[layer, :, columns]) + bqkv_ref[layer, group]).astype(jnp.bfloat16)
+            if i:
+                qkv_send[i - 1] = projected
+                q_copy(i).start()
+            else:
+                heads[layer, pl.ds(pl.multiple_of(s * rows, rows), rows), :] = projected
+        forward_on(m0 + 1)
+        for i in range(1, g):
+            q_arrival(i).wait_recv()
+        save(heads.at[layer], heads_out.at[layer])
+
+        def c_copy(i, b):
+            return pltpu.make_async_remote_copy(
+                src_ref=ctx_send.at[layer, i], dst_ref=ctx.at[layer, s],
+                send_sem=k_send_sem.at[layer, i], recv_sem=k_recv_sem.at[layer, i],
+                device_id={"fsdp": f, "seq": b}, device_id_type=MESH)
+
+        def attend(i, carry):
+            b = lax.rem(s + i, g)
+            block = pl.ds(pl.multiple_of(b * rows, rows), rows)
+            q_a = heads[layer, block, 0:128] * jnp.bfloat16(HD**-0.5)
+            q_d = heads[layer, block, 384:512] * jnp.bfloat16(HD**-0.5)
+            zero = jnp.zeros_like(q_a)
+            outs, logs = [], []
+            for h in range(3):
+                if h == 2:
+                    scores = dot_t(q_d, heads[layer, :, 512:640])
+                else:
+                    part = jnp.where(lane < 64, q_a, zero) if h == 0 else jnp.where(lane < 64, zero, q_a)
+                    scores = dot_t(part, heads[layer, :, 128:256])
+                scores = scores + mask_ref[...]
+                top = jnp.max(scores, axis=-1, keepdims=True)
+                exponent = jnp.exp(scores - top)
+                total = jnp.sum(exponent, axis=-1, keepdims=True)
+                values = heads[layer, :, 384:512] if h == 2 else heads[layer, :, 256:384]
+                outs.append(dot(exponent.astype(jnp.bfloat16), values) * (1.0 / total))
+                logs.append(top + jnp.log(total))
+            lse[layer, block, :] = jnp.where(lane == 0, logs[0], jnp.where(lane == 1, logs[1], logs[2]))
+            first = jnp.where(lane < 64, outs[0], outs[1]).astype(jnp.bfloat16)
+            second = jnp.where(lane < 64, 0.0, outs[2]).astype(jnp.bfloat16)
+
+            @pl.when(i < g)
+            def _():
+                ctx_send[layer, i, :, 0:128] = first
+                ctx_send[layer, i, :, 128:256] = second
+                c_copy(i, b).start()
+
+            @pl.when(i == g)
+            def _():
+                ctx[layer, s, :, 0:128] = first
+                ctx[layer, s, :, 128:256] = second
+
+            return carry
+
+        lax.fori_loop(1, g + 1, attend, 0)
+        save(lse.at[layer], lse_out.at[layer])
+        need(m0 + 1)
+        forward_on(m0 + 2)
+        for i in range(1, g):
+            pltpu.make_async_remote_copy(
+                src_ref=ctx_send.at[layer, i], dst_ref=ctx.at[layer, lax.rem(s - i + g, g)],
+                send_sem=k_send_sem.at[layer, i], recv_sem=k_recv_sem.at[layer, i],
+                device_id={"fsdp": f, "seq": lax.rem(s + i, g)}, device_id_type=MESH).wait_recv()
+        save(ctx.at[layer], ctx_out.at[layer])
+
+        total = x_s[...] + vec_ref[layer, B_OUT]
+        for grp in range(g):
+            base = grp * 3 * HD
+            total = total + dot(ctx[layer, grp, :, 0:128], wo[layer, base : base + 128, :])
+            total = total + dot(ctx[layer, grp, :, 128:256], wo[layer, base + 64 : base + 192, :])
+        r1[layer] = total
+        save(r1.at[layer], r1_out.at[layer])
+        normed = standardize(total)[0] * vec_ref[layer, GAIN_A] + vec_ref[layer, SHIFT_A]
+        nb_s[...] = normed.astype(jnp.bfloat16)
+        acc_s[...] = normed + vec_ref[layer, B_DOWN]
+        need(m0 + 2)
+        forward_on(m0 + 3)
+        need(m0 + 3)
+
+        def ffn(c, carry):
+            columns = pl.ds(pl.multiple_of(c * D, 128), D)
+            up = dot(nb_s[...], wu[layer, :, columns]) + vec_ref[layer, B_UP + c]
+            pre[layer, :, columns] = up
+            active = (up * (lax.erf(up * (0.5**0.5)) + 1.0) * 0.5).astype(jnp.bfloat16)
+            act[layer, :, columns] = active
+            acc_s[...] += dot(active, wd[layer, columns, :])
+            return carry
+
+        lax.fori_loop(0, FF // D, ffn, 0)
+        save(pre.at[layer], pre_out.at[layer])
+        save(act.at[layer], act_out.at[layer])
+        r2[layer] = acc_s[...]
+        save(r2.at[layer], r2_out.at[layer])
+        x_s[...] = standardize(acc_s[...])[0] * vec_ref[layer, GAIN_F] + vec_ref[layer, SHIFT_F]
+    y_ref[...] = x_s[...]
+
+    for m in range(4 * LAYERS):
+        for j in range(1, half):
+            to_chip(m, j).wait_send()
+        for j in range(half):
+            to_core(m, j).wait_send()
+        save_full(m).wait()
+    for i in range(1, g):
+        pltpu.make_async_remote_copy(
+            src_ref=qkv_send.at[i - 1], dst_ref=heads.at[LAYERS - 1, pl.ds(pl.multiple_of(s * rows, rows), rows)],
+            send_sem=q_send_sem.at[LAYERS - 1, i - 1], recv_sem=q_recv_sem.at[LAYERS - 1, i - 1],
+            device_id={"fsdp": f, "seq": lax.rem(s + i, g)}, device_id_type=MESH).wait_send()
+    for layer in range(LAYERS):
+        for i in range(1, g):
+            pltpu.make_async_remote_copy(
+                src_ref=ctx_send.at[layer, i], dst_ref=ctx.at[layer, s],
+                send_sem=k_send_sem.at[layer, i], recv_sem=k_recv_sem.at[layer, i],
+                device_id={"fsdp": f, "seq": lax.rem(s + i, g)}, device_id_type=MESH).wait_send()
+    for copy in saves:
+        copy.wait()
+
+
+def run_forward(n, g, x0, mask, bqkv, vecs, sq, so, su, sd):
+    rows, span = x0.shape[0], x0.shape[0] * g
+    any_spec = pl.BlockSpec(memory_space=pl.ANY)
+    vmem = pl.BlockSpec(memory_space=pltpu.VMEM)
+    bf, f32 = jnp.bfloat16, jnp.float32
+    half = n // 2
+    shapes = [
+        ((rows, D), f32, vmem),
+        ((LAYERS, D, g * GROUP), bf, any_spec),
+        ((LAYERS, D, D), bf, any_spec),
+        ((LAYERS, D, FF), bf, any_spec),
+        ((LAYERS, FF, D), bf, any_spec),
+        ((LAYERS, rows, D), bf, any_spec),
+        ((LAYERS, span, GROUP), bf, any_spec),
+        ((LAYERS, span, 128), f32, any_spec),
+        ((LAYERS, g, rows, CTX), bf, any_spec),
+        ((LAYERS, rows, D), f32, any_spec),
+        ((LAYERS, rows, FF), f32, any_spec),
+        ((LAYERS, rows, FF), bf, any_spec),
+        ((LAYERS, rows, D), f32, any_spec),
+    ]
+    dma = pltpu.SemaphoreType.DMA
+    return pl.pallas_call(
+        functools.partial(forward_kernel, n, g),
+        name="forward",
+        out_shape=[jax.ShapeDtypeStruct(a, b) for a, b, _ in shapes],
+        in_specs=[vmem] * 4 + [any_spec] * 4,
+        out_specs=[c for _, _, c in shapes],
+        scratch_shapes=[
+            pltpu.VMEM((LAYERS, D, g * GROUP), bf),
+            pltpu.VMEM((LAYERS, D, D), bf),
+            pltpu.VMEM((LAYERS, D, FF), bf),
+            pltpu.VMEM((LAYERS, FF, D), bf),
+            pltpu.VMEM((rows, D), f32),
+            pltpu.VMEM((LAYERS, rows, D), bf),
+            pltpu.VMEM((LAYERS, span, GROUP), bf),
+            pltpu.VMEM((LAYERS, span, 128), f32),
+            pltpu.VMEM((LAYERS, g, rows, CTX), bf),
+            pltpu.VMEM((LAYERS, rows, D), f32),
+            pltpu.VMEM((LAYERS, rows, FF), f32),
+            pltpu.VMEM((LAYERS, rows, FF), bf),
+            pltpu.VMEM((LAYERS, rows, D), f32),
+            pltpu.VMEM((rows, D), f32),
+            pltpu.VMEM((rows, D), bf),
+            pltpu.VMEM((g - 1, rows, GROUP), bf),
+            pltpu.VMEM((LAYERS, g, rows, CTX), bf),
+            dma((4 * LAYERS, half - 1)),
+            dma((4 * LAYERS, half - 1)),
+            dma((4 * LAYERS, half)),
+            dma((4 * LAYERS, half)),
+            dma((4 * LAYERS,)),
+            dma((LAYERS, g - 1)),
+            dma((LAYERS, g - 1)),
+            dma((LAYERS, g)),
+            dma((LAYERS, g)),
+            dma((8 * LAYERS,)),
+        ],
+        compiler_params=pltpu.CompilerParams(
+            collective_id=0, has_side_effects=True, vmem_limit_bytes=62 * 1024 * 1024
+        ),
+    )(x0, mask, bqkv, vecs, sq, so, su, sd)
+
+
+def group_columns(w, g):
+    lead = w.shape[:-1]
+    q, k, v = (w[..., i * D : (i + 1) * D].reshape(lead + (g, 3 * HD)) for i in range(3))
+    return jnp.concatenate(
+        [q[..., :128], k[..., :128], v[..., :128], q[..., 128:], v[..., 128:], k[..., 128:], jnp.zeros_like(k[..., 128:])], axis=-1)
+
+
+def ungroup_columns(w):
+    lead, g = w.shape[:-2], w.shape[-2]
+    q = jnp.concatenate([w[..., 0:128], w[..., 384:448]], axis=-1).reshape(lead + (D,))
+    k = jnp.concatenate([w[..., 128:256], w[..., 512:576]], axis=-1).reshape(lead + (D,))
+    v = jnp.concatenate([w[..., 256:384], w[..., 448:512]], axis=-1).reshape(lead + (D,))
+    return jnp.concatenate([q, k, v], axis=-1)
+
+
+def gather_vectors(n, g, b_qv, b_out, gain_attn, shift_attn, b_up, b_down, gain_ffn, shift_ffn):
+    width = D // n
+    packed = jnp.concatenate(
+        [b_qv.reshape(LAYERS, 2, width), b_out[:, None], gain_attn[:, None], shift_attn[:, None],
+         b_up.reshape(LAYERS, FF // D, width), b_down[:, None], gain_ffn[:, None], shift_ffn[:, None]], axis=1)
+    whole = lax.all_gather(packed, "fsdp", axis=0).astype(jnp.float32)
+    b = whole[:, :, 0:2].transpose(1, 0, 2, 3).reshape(LAYERS, 2 * D)
+    up = whole[:, :, 5:9].transpose(1, 0, 2, 3).reshape(LAYERS, FF // D, D)
+    rest = whole.transpose(1, 2, 0, 3).reshape(LAYERS, 12, D)
+    vecs = jnp.concatenate([rest[:, 2:5], up, rest[:, 9:12]], axis=1)[:, :, None]
+    full = jnp.concatenate([b[:, :D], jnp.zeros_like(b[:, :D]), b[:, D:]], axis=-1)
+    return group_columns(full, g)[:, :, None], vecs
 
 
 def norm_rows(values, gain_vec, shift_vec):
@@ -396,7 +742,7 @@
     return (weights_sum, smalls[8])
 
 
-def body(
+def plain_body(
     tokens,
     memory,
     lengths,
@@ -463,6 +809,92 @@
     return (result, grad_tokens, memory_sum) + tuple(summed)
 
 
+def kernel_backward(grad_output, weights, vecs, stored, key_live):
+    wq, wo, wu, wd = weights
+    xb, heads, lse, ctx, r1, pre, act, r2 = stored
+    g = ctx.shape[0]
+    rows = xb.shape[0]
+    gain_ffn, gain_attn, shift_attn = vecs[GAIN_F], vecs[GAIN_A], vecs[SHIFT_A]
+
+    def norm_backward(grad, residual, gain):
+        standard, scale = standardize(residual)
+        inner = grad * gain
+        back = scale * (inner - jnp.mean(inner, -1, keepdims=True) - standard * jnp.mean(inner * standard, -1, keepdims=True))
+        return back, jnp.sum(grad * standard, 0), jnp.sum(grad, 0), standard
+
+    grad_two, grad_gain_ffn, grad_shift_ffn, _ = norm_backward(grad_output, r2, gain_ffn)
+    branch = grad_two.astype(jnp.bfloat16)
+    grad_b_down = jnp.sum(branch.astype(jnp.float32), 0)
+    grad_w_down = t_dot(act, branch)
+    grad_active = dot_t(branch, wd)
+    slope = 0.5 * (lax.erf(pre * 0.5**0.5) + 1.0) + pre * jnp.exp(-0.5 * pre * pre) * (0.5 / math.pi) ** 0.5
+    grad_pre = (grad_active * slope).astype(jnp.bfloat16)
+    grad_b_up = jnp.sum(grad_pre.astype(jnp.float32), 0)
+    standard = standardize(r1)[0]
+    normed_low = (standard * gain_attn + shift_attn).astype(jnp.bfloat16)
+    grad_w_up = t_dot(normed_low, grad_pre)
+    grad_normed = dot_t(grad_pre, wu) + grad_two
+    grad_one, grad_gain_attn, grad_shift_attn, _ = norm_backward(grad_normed, r1, gain_attn)
+    attended = grad_one.astype(jnp.bfloat16)
+    grad_b_out = jnp.sum(attended.astype(jnp.float32), 0)
+    ctx_rows = jnp.concatenate([ctx[..., :128], ctx[..., 192:]], -1).transpose(1, 0, 2).reshape(rows, D)
+    grad_w_out = t_dot(ctx_rows, attended)
+    grad_ctx = dot_t(attended, wo).astype(jnp.bfloat16).reshape(rows, g, 3, HD)
+    grad_heads = lax.all_to_all(grad_ctx, "seq", split_axis=1, concat_axis=0, tiled=True)[:, 0]
+    q = jnp.concatenate([heads[:, 0:128], heads[:, 384:448]], -1).reshape(-1, 3, HD)
+    k = jnp.concatenate([heads[:, 128:256], heads[:, 512:576]], -1).reshape(-1, 3, HD)
+    v = jnp.concatenate([heads[:, 256:384], heads[:, 448:512]], -1).reshape(-1, 3, HD)
+    log_total = jnp.moveaxis(lse[:, :3].reshape(2, -1, 3), 2, 1)
+    gq, gk, gv = attend_backward(q, k, v, grad_heads, log_total, key_live)
+    stack = jnp.stack([gq, gk, gv], 1).astype(jnp.bfloat16)[:, :, None]
+    projected = lax.all_to_all(stack, "seq", split_axis=0, concat_axis=2, tiled=True).reshape(rows, 3 * D)
+    sums = jnp.sum(projected.astype(jnp.float32), 0)
+    grad_b_qv = jnp.concatenate([sums[:D], sums[2 * D :]])
+    grad_w_qkv = t_dot(xb, projected)
+    w_full = ungroup_columns(wq.reshape(D, g, GROUP))
+    grad_hidden = dot_t(projected, w_full) + grad_one
+    return grad_hidden, (grad_w_qkv, grad_b_qv, grad_w_out, grad_b_out, grad_gain_attn, grad_shift_attn, grad_w_up, grad_b_up,
+                         grad_w_down, grad_b_down, grad_gain_ffn, grad_shift_ffn)
+
+
+def kernel_body(
+    tokens, memory, lengths, w_qkv, b_qv, w_out, b_out, gain_attn, shift_attn, w_up, b_up, w_down, b_down, gain_ffn, shift_ffn, cotangent,
+):
+    local_rows = tokens.shape[0]
+    n, g = lax.axis_size("fsdp"), lax.axis_size("seq")
+    positions = lax.axis_index("seq") * local_rows + jnp.arange(local_rows, dtype=jnp.int32)
+    length = lengths[0]
+    key_live = jnp.arange(local_rows * g, dtype=jnp.int32) < length + 2 * MEM
+    row_live = (positions < length + 2 * MEM)[:, None]
+    token_live = ((positions >= MEM) & (positions < length + MEM))[:, None]
+    memory_slots = jnp.arange(2 * MEM, dtype=jnp.int32)
+    targets = jnp.where(memory_slots < MEM, memory_slots, length + memory_slots)
+    select = positions[:, None] == targets[None, :]
+    x0 = jnp.where(token_live, tokens.astype(jnp.float32), 0.0) + dot(select.astype(jnp.bfloat16), memory[0])
+    mask = jnp.where(key_live, 0.0, masked_score)[None].astype(jnp.float32)
+    bqkv, vecs = gather_vectors(n, g, b_qv, b_out, gain_attn, shift_attn, b_up, b_down, gain_ffn, shift_ffn)
+    sq = group_columns(w_qkv, g).reshape(LAYERS, w_qkv.shape[1], g * GROUP)
+    y, fq, fo, fu, fd, *stored = run_forward(n, g, x0, mask, bqkv, vecs, sq, w_out, w_up, w_down)
+    result = jnp.where(row_live, y, 0.0)
+    grad_hidden = jnp.where(row_live, cotangent, 0.0)
+    collected = []
+    for layer in reversed(range(LAYERS)):
+        grad_hidden, grads = kernel_backward(
+            grad_hidden, (fq[layer], fo[layer], fu[layer], fd[layer]), vecs[layer, :, 0], [item[layer] for item in stored], key_live)
+        collected.insert(0, fsdp_layer_sum(grads))
+    stacked = tuple(jnp.stack(member) for member in zip(*collected))
+    grad_tokens = jnp.where(token_live, grad_hidden, 0.0)
+    grad_memory = jnp.dot(select.astype(jnp.float32).T, grad_hidden, precision=lax.Precision.HIGHEST)[None]
+    summed, memory_sum = seq_total_sum(stacked, grad_memory)
+    return (result, grad_tokens, memory_sum) + tuple(summed)
+
+
+def pick_body(mesh):
+    n, g = mesh.shape["fsdp"], mesh.shape["seq"]
+    fits = n % 2 == 0 and (D // n) % 32 == 0 and HEADS == 3 * g
+    return kernel_body if fits else plain_body
+
+
 def solution(mesh):
     in_specs = (
         P(("fsdp", "seq"), None),
@@ -499,4 +931,4 @@
         P(None, "fsdp"),
         P(None, "fsdp"),
     )
-    return jax.shard_map(body, mesh=mesh, in_specs=in_specs, out_specs=out_specs, check_vma=False)
+    return jax.shard_map(pick_body(mesh), mesh=mesh, in_specs=in_specs, out_specs=out_specs, check_vma=False)

time: 1050 us -> 942 us (0.90)
  waiting for transfers between devices: 502 us -> 308 us
  Pallas kernels: 0 us -> 174 us
  matrix products: 157 us -> 104 us
  blocking collectives: 172 us -> 142 us
  local copies, waits for them, and re-layouts: 107 us -> 126 us
  starting transfers between devices: 30.3 us -> 12.3 us
    pallas_call x0 -> x1, Pallas kernels: none -> 174 us  [run_forward(): pl.pallas_call(functools.partial(forward_kernel, n, g), name='forward', o...]
    all_to_all x7 -> x3, waiting for transfers between devices: 101 us -> 10.4 us  [the longest x1 8.35 us: kernel_backward(): lax.all_to_all(stack, 'seq', split_axis=0, concat_axis=2, tiled=True)]
    all_gather x8 -> x0, waiting for transfers between devices: 81.1 us -> none  [the longest x2 49.4 us: gather_layer(): lax.all_gather(w_down, 'fsdp', axis=0, tiled=True)]
    dot_general x30 -> x18, matrix products: 106 us -> 58.8 us  [the longest x8 31.4 us: t_dot(): lax.dot_general(a, b, (((0,), (0,)), ((), ())), preferred_element_type=jn...]
    unnamed x2 -> x1, blocking collectives: 51.8 us -> 26.1 us
    unnamed x25 -> x17, waiting for transfers between devices: 64.5 us -> 46.6 us
    all_to_all x7 -> x3, starting transfers between devices: 28.9 us -> 11.1 us  [the longest x2 7.57 us: kernel_backward(): lax.all_to_all(grad_ctx, 'seq', split_axis=1, concat_axis=0, tiled=True)]
    unnamed x331 -> x169, local copies, waits for them, and re-layouts: 53.7 us -> 39 us
  transfers between devices with their start and end apart: 29 -> 17, of which waited for: 18 -> 13; matrix products, arithmetic and copies ran while one was open for 23% -> 26% of each run, Pallas kernels for 0% -> 0%
where the time goes in v2:
time: 942 us; the launch traced here: 937 us
  waiting for transfers between devices  308 us (33%)
  Pallas kernels  174 us (18%)
  blocking collectives  142 us (15%)
  local copies, waits for them, and re-layouts  126 us (13%)
  matrix products  104 us (11%)
  other arithmetic  51.1 us (5%)
  between operations  18.9 us (2%)
  starting transfers between devices  12.3 us (1%)
    pallas_call x1, Pallas kernels, run_forward(): pl.pallas_call(functools.partial(forward_kernel, n, g), name='forward', o...  174 us
    reduce_scatter x2, waiting for transfers between devices, fsdp_layer_sum(): lax.psum_scatter(grad_w_up.astype(jnp.bfloat16), 'fsdp', scatter_dimensio...  110 us
    reduce_scatter x2, waiting for transfers between devices, fsdp_layer_sum(): lax.psum_scatter(grad_w_qkv.astype(jnp.bfloat16), 'fsdp', scatter_dimensi...  94.5 us
    unnamed x17, waiting for transfers between devices  46.6 us
    unnamed x169, local copies, waits for them, and re-layouts  39 us
    all_gather x1, blocking collectives, seq_total_sum(): lax.all_gather(pieces[0].astype(jnp.bfloat16), 'seq', axis=2, tiled=True)  35.9 us
    all_to_all x1, blocking collectives, kernel_backward(): lax.all_to_all(stack, 'seq', split_axis=0, concat_axis=2, tiled=True)  32.4 us
    dot_general x8, matrix products, t_dot(): lax.dot_general(a, b, (((0,), (0,)), ((), ())), preferred_element_type=jn...  31.4 us
  transfers between devices with their start and end apart: 17, of which 13 were waited for; matrix products, arithmetic and copies ran while one was open for 26% of the time, Pallas kernels for 0%

profile of v2, /device:TPU:0, one launch (start us, length us, event | category | flops | bytes accessed | tf_op | source)
XLA Modules:
  0.0 937.0 jit_solution(477790528758758704)
XLA Ops:
  10.5 10.7 %all-gather = bf16[16,12,96]{2,1,0:T(8,128)(2,1)S(1)} all-gather(bf16[2,12,96]{2,1,0:T(8,128)(2,1)S(1)} %concatenate.84), channel_id=2, replica_groups=mesh['fsdp'=8,'seq'=4] {'fsdp'}, dimensions={0}, use_global_device_ids=true | all-gather | bytes 41472 | tf_op jit(solution)/shard_map/all_gather | solution.py:356
  22.5 4.6 concatenate.87
  32.6 174.1 %forward.1 = (f32[256,768]{1,0:T(8,128)}, bf16[2,768,2560]{2,1,0:T(8,128)(2,1)}, bf16[2,768,768]{2,1,0:T(8,128)(2,1)}, bf16[2,768,3072]{2,1,0:T(8,128)(2,1)}, bf...) custom-call(f32[256,768]{1,0:T(8,128)} %convolution_add_fusion.refs_, ...), custom_call_target="tpu_custom_call" | custom-call | tf_op jit(solution)/shard_map/forward/pallas_call | solution.py:295
  209.8 3.2 multiply_reduce_fusion.2
  214.4 5.1 fusion.181
  224.1 4.1 all-to-all-start
  243.3 27.6 %while.30 = (s32[]{:T(128)}, f32[1024,3,64]{0,2,1:T(8,128)}, f32[1024,3,64]{0,2,1:T(8,128)}, bf16[2,512,3,64]{1,3,2,0:T(8,128)(2,1)}, bf16[2,512,3,64]{1,3,2,0:T...) while((s32[]{:T(128)}, f32[1024,3,64]{0,2,1:T(8,128)}, ...), condition=%wide.region_14.15_spmd.clone, body=%wide.region_12.14_spmd.clone.sunk | while | flops 1031306752 | bytes 112617472 | solution.py:478
  253.6 3.4 fusion.241
  267.2 3.7 fusion.241
  275.1 4.6 copy.317
  279.7 3.1 reshape.424
  282.7 3.5 all-to-all-start.1
  286.3 5.6 fusion.167
  292.1 6.3 copy.362
  306.6 8.3 all-to-all-done.1
  314.9 3.2 reshape.425
  318.1 4.8 copy.356
  323.2 4.7 multiply_reduce_fusion.3
  328.8 5.3 fusion.182
  339.0 5.1 convolution_convert_fusion
  345.2 5.0 convolution_convert_fusion.1
  350.9 5.2 convolution_convert_fusion.2
  356.7 5.3 convolution_convert_fusion.3
  368.2 3.5 all-to-all-start.2
  386.4 27.5 %while.31 = (s32[]{:T(128)}, f32[1024,3,64]{0,2,1:T(8,128)}, f32[1024,3,64]{0,2,1:T(8,128)}, bf16[2,512,3,64]{1,3,2,0:T(8,128)(2,1)}, bf16[2,512,3,64]{1,3,2,0:T...) while((s32[]{:T(128)}, f32[1024,3,64]{0,2,1:T(8,128)}, ...), condition=%wide.region_21.22_spmd.clone, body=%wide.region_19.21_spmd.clone.sunk | while | flops 1031306752 | bytes 112510848 | solution.py:478
  396.4 3.4 fusion.254
  410.2 3.7 fusion.254
  418.1 4.6 copy.332
  422.8 3.1 reshape.426
  425.8 32.4 %all_to_all.60 = bf16[4,2,73728]{2,1,0:T(2,128)(2,1)} all-to-all(bf16[4,2,73728]{2,1,0:T(2,128)(2,1)} %reshape.426), channel_id=1, replica_groups=mesh['fsdp'=8,'seq'=4] {'seq'}, dimensions={0} | all-to-all | bytes 2359296 | tf_op jit(solution)/shard_map/all_to_all | solution.py:850
  458.3 3.5 reshape.427
  461.7 3.8 copy.357
  467.0 3.9 convolution_convert_fusion.5
  473.5 15.2 %reduce-scatter.30.cloned.1.call-done = bf16[384,768]{1,0:T(8,128)(2,1)} async-done(((bf16[3072,768]{1,0:T(8,128)(2,1)}), bf16[384,768]{1,0:T(8,128)(2,1)}) %reduce-scatter.30.cloned.1.call-update) | async-done | bytes 589840 | tf_op jit(solution)/shard_map/reduce_scatter | solution.py:667
  493.3 52.7 %reduce-scatter.26.cloned.1.call-done = bf16[96,3072]{1,0:T(8,128)(2,1)} async-done(((bf16[768,3072]{1,0:T(8,128)(2,1)}), bf16[96,3072]{1,0:T(8,128)(2,1)}) %reduce-scatter.26.cloned.1.call-update) | async-done | bytes 589840 | tf_op jit(solution)/shard_map/reduce_scatter | solution.py:665
  546.0 57.6 %reduce-scatter.24.cloned.1.call-done = bf16[96,3072]{1,0:T(8,128)(2,1)} async-done(((bf16[768,3072]{1,0:T(8,128)(2,1)}), bf16[96,3072]{1,0:T(8,128)(2,1)}) %reduce-scatter.24.cloned.1.call-update) | async-done | bytes 589840 | tf_op jit(solution)/shard_map/reduce_scatter | solution.py:665
  606.1 6.3 copy.363
  612.3 42.9 %reduce-scatter.18.cloned.1.call-done = bf16[96,2304]{1,0:T(8,128)(2,1)} async-done(((bf16[768,2304]{1,0:T(8,128)(2,1)}), bf16[96,2304]{1,0:T(8,128)(2,1)}) %reduce-scatter.18.cloned.1.call-update) | async-done | bytes 442384 | tf_op jit(solution)/shard_map/reduce_scatter | solution.py:659
  655.2 51.6 %reduce-scatter.16.cloned.1.call-done = bf16[96,2304]{1,0:T(8,128)(2,1)} async-done(((bf16[768,2304]{1,0:T(8,128)(2,1)}), bf16[96,2304]{1,0:T(8,128)(2,1)}) %reduce-scatter.16.cloned.1.call-update) | async-done | bytes 442384 | tf_op jit(solution)/shard_map/reduce_scatter | solution.py:659
  725.1 5.2 reduce-scatter.36.cloned.1.call-done
  731.9 17.9 %all_gather.21 = bf16[2,96,768]{1,0,2:T(2,128)(2,1)S(1)} all-gather(bf16[2,96,192]{1,0,2:T(2,128)(2,1)} %bitcast.436), channel_id=1, replica_groups=mesh['fsdp'=8,'seq'=4] {'seq'}, dimensions={2}, use_global_device_ids=true | all-gather | bytes 368640 | tf_op jit(solution)/shard_map/all_gather | solution.py:707
  751.7 38.7 %all-reduce.21.cloned.1.call-done = bf16[2,384,768]{1,0,2:T(2,128)(2,1)} async-done(((bf16[2,384,768]{1,0,2:T(2,128)(2,1)}), bf16[2,384,768]{1,0,2:T(2,128)(2,1)}) %all-reduce.21.cloned.1.call-update) | async-done | bytes 1179664
  792.8 26.1 %all-reduce.17 = (bf16[1536]{0:T(1024)(128)(2,1)S(1)}, bf16[1536]{0:T(1024)(128)(2,1)S(1)}, bf16[768]{0:T(1024)(128)(2,1)S(1)}, bf16[768]{0:T(1024)(128)(2,1)S(1...) all-reduce(bf16[1536]{0:T(1024)(128)(2,1)S(1)} %pad_maximum_fusion., ...), channel_id=7, replica_groups=mesh['fsdp'=8,'seq'=4] {'fsdp'}, use_global_device_ids=true, to_apply=%region_29.30.clone | all-reduce | flops 18432 | bytes 73728
  821.7 4.0 broadcast_select_fusion
  826.2 19.2 %all-reduce.18 = (bf16[1,20,768]{2,1,0:T(8,128)(2,1)S(1)}, bf16[2,192]{1,0:T(2,128)(2,1)S(1)}, bf16[2,96]{1,0:T(2,128)(2,1)S(1)}, bf16[2,96]{1,0:T(2,128)(2,1)S(...) all-reduce(bf16[1,20,768]{2,1,0:T(8,128)(2,1)S(1)} %fusion.134, ...), channel_id=1, replica_groups=mesh['fsdp'=8,'seq'=4] {'seq'}, use_global_device_ids=true, to_apply=%region_22.23 | all-reduce | flops 17664 | bytes 70656 | tf_op jit(solution)/shard_map/psum | solution.py:726
  854.2 35.9 %all_gather.20 = bf16[2,96,2304]{1,0,2:T(2,128)(2,1)S(1)} all-gather(bf16[2,96,576]{1,0,2:T(2,128)(2,1)S(1)} %bitcast.427), channel_id=1, replica_groups=mesh['fsdp'=8,'seq'=4] {'seq'}, dimensions={2}, use_global_device_ids=true | all-gather | bytes 1105920 | tf_op jit(solution)/shard_map/all_gather | solution.py:704
  895.4 5.1 copy.353
  900.5 26.9 %all-gather.4.cloned.1.call-done = bf16[2,96,3072]{2,1,0:T(8,128)(2,1)} async-done(((bf16[2,96,768]{2,1,0:T(8,128)(2,1)}), bf16[2,96,3072]{2,1,0:T(8,128)(2,1)}) %all-gather.4.cloned.1.call-update) | async-done | bytes 1179664 | tf_op jit(solution)/shard_map/all_gather | solution.py:710
  (512 shorter events, 171.3 us)
Async XLA Ops:
  7.2 24.2 %copy-start = (bf16[1,20,768]{2,1,0:T(8,128)(2,1)S(1)}, bf16[1,20,768]{2,1,0:T(8,128)(2,1)}, u32[]{:S(2)}) copy-start(bf16[1,20,768]{2,1,0:T(8,128)(2,1)} %param.21) | copy-start | bytes 92164
  21.2 10.2 %copy-start.48 = (bf16[256,768]{1,0:T(8,128)(2,1)S(1)}, bf16[256,768]{1,0:T(8,128)(2,1)}, u32[]{:S(2)}) copy-start(bf16[256,768]{1,0:T(8,128)(2,1)} %param.20) | copy-start | bytes 1179652
  32.6 177.2 %copy-start.34 = (f32[256,768]{1,0:T(8,128)S(1)}, f32[256,768]{1,0:T(8,128)}, u32[]{:S(2)}) copy-start(f32[256,768]{1,0:T(8,128)} %param.35) | copy-start | bytes 2359300
  206.7 6.4 copy-start.8
  213.2 8.6 copy-start.55
  213.4 8.3 copy-start.60
  213.5 6.0 copy-start.58
  213.5 6.0 slice-start
  214.4 5.1 copy-start.35
  214.4 5.1 slice-start.1
  214.4 5.1 slice-start.2
  221.8 6.5 copy-start.47
  222.7 9.6 %copy-start.25 = (f32[256,768]{1,0:T(8,128)}, f32[256,768]{1,0:T(8,128)S(1)}, u32[]{:S(2)}) copy-start(f32[256,768]{1,0:T(8,128)S(1)} %get-tuple-element.572) | copy-start | bytes 2359300
  224.1 16.8 %all-to-all-start = ((bf16[256,4,3,64]{0,3,2,1:T(8,128)(2,1)}), bf16[256,4,3,64]{0,3,2,1:T(8,128)(2,1)}, u32[]{:S(2)}, u32[]{:S(2)}) async-start(bf16[256,4,3,64]{0,3,2,1:T(8,128)(2,1)} %bitcast.32), calls=%async_computation | async-start | bytes 786432 | tf_op jit(solution)/shard_map/all_to_all | solution.py:843
  228.2 242.8 %reduce-scatter.22.cloned.1.call-start = ((), (), s32[]{:S(2)}) async-start(), calls=%async_computation.18 | async-start | bytes 1327104 | tf_op jit(solution)/shard_map/reduce_scatter | solution.py:661
  229.2 5.6 copy-start.39
  282.7 32.2 %all-to-all-start.1 = ((bf16[4,2,73728]{2,1,0:T(2,128)(2,1)}), bf16[4,2,73728]{2,1,0:T(2,128)(2,1)S(1)}, u32[]{:S(2)}, u32[]{:S(2)}) async-start(bf16[4,2,73728]{2,1,0:T(2,128)(2,1)} %reshape.424), calls=%async_computation.1 | async-start | bytes 2359296 | tf_op jit(solution)/shard_map/all_to_all | solution.py:850
  286.3 184.8 %reduce-scatter.20.cloned.1.call-start = ((), (), s32[]{:S(2)}) async-start(), calls=%async_computation.17 | async-start | bytes 1327104 | tf_op jit(solution)/shard_map/reduce_scatter | solution.py:661
  286.3 5.6 copy-start.42
  318.1 5.1 copy-start.57
  323.2 10.9 %slice-start.3 = ((s8[9437184]{0:T(1024)(128)(4,1)}), s8[4194304]{0:T(1024)(128)(4,1)S(1)}, s32[]{:S(2)}) async-start(s8[9437184]{0:T(1024)(128)(4,1)} %bitcast.443), calls=%async_computation.32 | async-start | bytes 8388608
  323.2 10.9 %slice-start.4 = ((s8[9437184]{0:T(1024)(128)(4,1)}), s8[4194304]{0:T(1024)(128)(4,1)S(1)}, s32[]{:S(2)}) async-start(s8[9437184]{0:T(1024)(128)(4,1)} %bitcast.443), calls=%async_computation.33 | async-start | bytes 8388608
  328.8 5.3 copy-start.37
  328.8 5.3 copy-start.9
  328.8 5.3 copy-start.59
  328.8 5.3 slice-start.5
  337.4 28.1 %copy-start.23 = (f32[256,768]{1,0:T(8,128)}, f32[256,768]{1,0:T(8,128)S(1)}, u32[]{:S(2)}) copy-start(f32[256,768]{1,0:T(8,128)S(1)} %get-tuple-element.570) | copy-start | bytes 2359300
  338.9 134.6 %reduce-scatter.32.cloned.1.call-start = ((), (), s32[]{:S(2)}) async-start(), calls=%async_computation.24 | async-start | bytes 5308416 | tf_op jit(solution)/shard_map/reduce_scatter | solution.py:667
  344.1 144.7 %reduce-scatter.30.cloned.1.call-start = ((), (), s32[]{:S(2)}) async-start(), calls=%async_computation.23 | async-start | bytes 5308416 | tf_op jit(solution)/shard_map/reduce_scatter | solution.py:667
  350.2 195.8 %reduce-scatter.26.cloned.1.call-start = ((), (), s32[]{:S(2)}) async-start(), calls=%async_computation.20 | async-start | bytes 5308416 | tf_op jit(solution)/shard_map/reduce_scatter | solution.py:665
  356.1 247.5 %reduce-scatter.24.cloned.1.call-start = ((), (), s32[]{:S(2)}) async-start(), calls=%async_computation.19 | async-start | bytes 5308416 | tf_op jit(solution)/shard_map/reduce_scatter | solution.py:665
  368.2 16.8 %all-to-all-start.2 = ((bf16[256,4,3,64]{0,3,2,1:T(8,128)(2,1)}), bf16[256,4,3,64]{0,3,2,1:T(8,128)(2,1)S(1)}, u32[]{:S(2)}, u32[]{:S(2)}) async-start(bf16[256,4,3,64]{0,3,2,1:T(8,128)(2,1)} %bitcast.48), calls=%async_computation.2 | async-start | bytes 786432 | tf_op jit(solution)/shard_map/all_to_all | solution.py:843
  371.7 10.3 %copy-start.33 = (bf16[256,3,4,1,3,64]{0,5,4,2,1,3:T(8,128)(2,1)S(1)}, bf16[256,3,4,1,3,64]{0,5,4,2,1,3:T(8,128)(2,1)}, u32[]{:S(2)}) copy-start(bf16[256,3,4,1,3,64]{0,5,4,2,1,3:T(8,128)(2,1)} %copy-done.32) | copy-start | bytes 3538948
  371.7 10.3 %copy-start.41 = (bf16[2,256,768]{2,1,0:T(8,128)(2,1)S(1)}, bf16[2,256,768]{2,1,0:T(8,128)(2,1)}, u32[]{:S(2)}) copy-start(bf16[2,256,768]{2,1,0:T(8,128)(2,1)} %get-tuple-element.152) | copy-start | bytes 2359300
  371.7 283.5 %reduce-scatter.18.cloned.1.call-start = ((), (), s32[]{:S(2)}) async-start(), calls=%async_computation.16 | async-start | bytes 3981312 | tf_op jit(solution)/shard_map/reduce_scatter | solution.py:659
  384.9 321.9 %reduce-scatter.16.cloned.1.call-start = ((), (), s32[]{:S(2)}) async-start(), calls=%async_computation.15 | async-start | bytes 3981312 | tf_op jit(solution)/shard_map/reduce_scatter | solution.py:659
  470.9 259.3 %reduce-scatter.36.cloned.1.call-start = ((), (), s32[]{:S(2)}) async-start(), calls=%async_computation.27 | async-start | bytes 491520
  473.5 316.9 %all-reduce.21.cloned.1.call-start = ((), (), s32[]{:S(2)}) async-start(), calls=%async_computation.28 | async-start | bytes 2359296
  493.1 328.5 %reduce-scatter.28.cloned.1.call-start = ((), (), s32[]{:S(2)}) async-start(), calls=%async_computation.21 | async-start | bytes 1474560 | tf_op jit(solution)/shard_map/reduce_scatter | solution.py:696
  606.0 247.1 %reduce-scatter.34.cloned.1.call-start = ((), (), s32[]{:S(2)}) async-start(), calls=%async_computation.26 | async-start | bytes 1474560
  713.6 181.8 %all-gather.6.cloned.1.call-start = ((), (), s32[]{:S(2)}) async-start(), calls=%async_computation.25 | async-start | bytes 1474560 | tf_op jit(solution)/shard_map/all_gather | solution.py:713
  722.8 28.1 %copy-start.22 = (bf16[4,256,3,1,3,64]{1,0,5,4,2,3:T(4,128)(2,1)S(1)}, bf16[4,256,3,1,3,64]{1,0,5,4,2,3:T(4,128)(2,1)}, u32[]{:S(2)}) copy-start(bf16[4,256,3,1,3,64]{1,0,5,4,2,3:T(4,128)(2,1)} %copy.357) | copy-start | bytes 3538948
  723.9 68.9 %copy-start.64 = (bf16[768]{0:T(1024)(128)(2,1)S(1)}, bf16[768]{0:T(1024)(128)(2,1)}, u32[]{:S(2)}) copy-start(bf16[768]{0:T(1024)(128)(2,1)} %get-tuple-element.472) | copy-start | bytes 4612
  723.9 68.9 %copy-start.65 = (bf16[768]{0:T(1024)(128)(2,1)S(1)}, bf16[768]{0:T(1024)(128)(2,1)}, u32[]{:S(2)}) copy-start(bf16[768]{0:T(1024)(128)(2,1)} %get-tuple-element.490) | copy-start | bytes 4612
  723.9 68.9 %copy-start.66 = (bf16[768]{0:T(1024)(128)(2,1)S(1)}, bf16[768]{0:T(1024)(128)(2,1)}, u32[]{:S(2)}) copy-start(bf16[768]{0:T(1024)(128)(2,1)} %get-tuple-element.567) | copy-start | bytes 4612
  723.9 97.8 %copy-start.24 = (f32[256,768]{1,0:T(8,128)S(1)}, f32[256,768]{1,0:T(8,128)}, u32[]{:S(2)}) copy-start(f32[256,768]{1,0:T(8,128)} %copy-done.23) | copy-start | bytes 2359300
  792.3 135.1 %all-gather.4.cloned.1.call-start = ((), (), s32[]{:S(2)}) async-start(), calls=%async_computation.22 | async-start | bytes 1474560 | tf_op jit(solution)/shard_map/all_gather | solution.py:710
  890.1 40.2 %copy-start.1 = (bf16[1,20,768]{2,1,0:T(8,128)(2,1)S(1)}, bf16[1,20,768]{2,1,0:T(8,128)(2,1)}, u32[]{:S(2)}) copy-start(bf16[1,20,768]{2,1,0:T(8,128)(2,1)} %param.21) | copy-start | bytes 92164
  (81 other events, 225.5 us)
Sparse Core Ops, SparseCore 0:
  234.9 36.4 reduce-scatter.21
  339.0 34.7 reduce-scatter.19
  377.3 53.8 reduce-scatter.31
  434.9 53.8 reduce-scatter.29
  492.1 53.8 reduce-scatter.25
  549.7 53.8 reduce-scatter.23
  607.1 48.0 reduce-scatter.17
  658.7 48.0 reduce-scatter.15
  709.7 20.5 reduce-scatter.35
  732.6 57.7 all-reduce.20
  792.8 28.7 reduce-scatter.27
  823.9 29.1 reduce-scatter.33
  854.7 40.6 all-gather.5
  896.9 30.3 all-gather.3
